TPU v7x, 512 devices: a whole 4x8x8 slice. The times are simulated.
512 devices in a mesh: tm: 32 (over y, z_hi), gz: 4 (over z_lo, core), row: 4 (over x).
Axes of the slice: x: 4, y: 8, z: 8 (z_hi: 4, z_lo: 2; z = z_hi * 2 + z_lo), core: 2. Of those that a mesh axis runs over, the one named last changes fastest.
Arguments:
- starts: float32 [32, 6, 256, 2048], P('tm', None, 'row', 'gz'), may hold values from -6 to 6
- coarse_map: float32 [32, 36, 64, 512], P('tm', None, 'row', 'gz'), may hold values from -0.2 to 1, as said below
- diffusivity: float32 [6], replicated, may hold values from 0.5 to 1
Outputs:
- next_starts: float32 [32, 6, 256, 2048], P('tm', None, 'row', 'gz')
Inputs may be any that keep to these rules, and one draw needn't show every extreme that they name: `coarse_map`: in every coarse cell the absolute values of each row of the matrix sum to at most 0.99; diagonal entries are positive.
All inputs are finite; a program needn't handle non-finite values.
Results may differ from a plain program's by a relative error of at most 0.0001.
Values sent between devices are 32-bit elements; how exact they have to be, the bound alone decides.
No kernel may reach another device: no remote copies, remote signals or barrier semaphores. Data moves between devices by JAX's collectives and lax.ppermute only.
A program may use at most 64 MiB of HBM per device.

v0:
```python
import jax
import jax.numpy as jnp
from jax import lax
from jax.sharding import PartitionSpec as P

FSTEPS = 4


time_step = 0.24


def extended_2(value, sides, width):
    for axis, dim in sides:
        size, length = (lax.axis_size(axis), value.shape[dim])
        up = [(i, (i + 1) % size) for i in range(size - 1)]
        down = [(j, i) for i, j in up]
        last = lax.slice_in_dim(value, length - width, length, axis=dim)
        initial = lax.slice_in_dim(value, 0, width, axis=dim)
        before = lax.ppermute(last, axis, up)
        after = lax.ppermute(initial, axis, down)
        value = jnp.concatenate([before, value, after], axis=dim)
    return value


def passed_along(value, axis, steps):
    count = lax.axis_size(axis)
    initial, last = (max(0, -steps), min(count, count - steps))
    return lax.ppermute(value, axis, [(source, source + steps) for source in range(initial, last)])


def fine_step(padded, row_start, diffusivity):
    center = padded[:, 1:-1, 1:-1]
    height_rows = center.shape[1]
    speed = 0.25 * jnp.tanh(padded[1])
    east_cell = padded[:, 1:-1, 2:]
    west_cell = padded[:, 1:-1, :-2]
    north_cell = padded[:, 2:, 1:-1]
    south_cell = padded[:, :-2, 1:-1]
    speed_mid = speed[1:-1, 1:-1]
    eastward_flux = 0.25 * (speed_mid + speed[1:-1, 2:]) * (center + east_cell)
    flux_west = 0.25 * (speed_mid + speed[1:-1, :-2]) * (center + west_cell)
    radius = (row_start + jnp.arange(height_rows, dtype=jnp.int32)).astype(jnp.float32)[:, None]
    radial = ((radius + 1.0) * (north_cell - center) - radius * (center - south_cell)) / (
        radius + 0.5
    )
    spread_rate = diffusivity[:, None, None]
    change = spread_rate * (radial + east_cell - 2.0 * center + west_cell) - (
        eastward_flux - flux_west
    )
    return center + time_step * change


def restrict(field):
    count, height_rows, width_cols = field.shape
    return field.reshape(count, height_rows // 4, 4, width_cols // 4, 4).mean(axis=(2, 4))


def prolong(field):
    return jnp.repeat(jnp.repeat(field, 4, axis=1), 4, axis=2)


def apply_map(matrix, vector):
    return jnp.sum(matrix * vector[None], axis=1)


def local(starts, coarse_map, diffusivity):
    start_state = starts[0]
    height_rows = start_state.shape[1]
    row_start = lax.axis_index("row") * height_rows

    def one_step(turn_index, state):
        extended = extended_2(state, (("gz", 2), ("row", 1)), 1)
        return fine_step(extended, row_start, diffusivity)

    fine_state = lax.fori_loop(0, FSTEPS, one_step, start_state)
    later_state = passed_along(start_state, "tm", -1)
    later_coarse = restrict(later_state)
    jump = restrict(fine_state) - later_coarse
    matrix = coarse_map[0].reshape(6, 6, coarse_map.shape[2], coarse_map.shape[3])
    slice_index = lax.axis_index("tm")

    def relay_turn(turn_index, carry_now):
        outgoing = apply_map(matrix, carry_now) + jump
        incoming = passed_along(outgoing, "tm", 1)
        return jnp.where(slice_index == turn_index + 1, incoming, carry_now)

    carry = lax.fori_loop(0, lax.axis_size("tm") - 1, relay_turn, jnp.zeros_like(jump))
    result = fine_state + prolong(apply_map(matrix, carry))
    return result[None]


def solution(mesh):
    placed = (P("tm", None, "row", "gz"), P("tm", None, "row", "gz"), P())
    return jax.shard_map(
        local, mesh=mesh, in_specs=placed, out_specs=P("tm", None, "row", "gz"), check_vma=False
    )
```

profile of v0, /device:TPU:96, one launch (start us, length us, event | category | flops | bytes accessed | tf_op | source)
XLA Modules:
  0.0 514.0 jit_solution(17210300014927330460)
XLA Ops:
  0.0 10.0 %collective-permute-start.5 = (f32[6,64,512]{2,1,0:T(8,128)}, f32[6,64,512]{2,1,0:T(8,128)S(1)}, u32[]{:S(2)}, u32[]{:S(2)}) collective-permute-start(f32[6,64,512]{2,1,0:T(8,128)} %bitcast.12), channel_id=1, source_target_pairs={{16,0},{32,16},{48,32},{64,48},{80,64},{96,80},{112,96},{128,112},... | collective-permute-start | bytes 2359304 | tf_op jit(solution)/shard_map/ppermute | solution.py:28
  11.2 100.2 %while.24 = (s32[]{:T(128)}, f32[6,64,512]{2,1,0:T(8,128)S(1)}, f32[6]{0:T(128)S(1)}, s32[]{:T(128)}, s32[]{:T(128)}) while((s32[]{:T(128)}, f32[6,64,512]{2,1,0:T(8,128)S(1)}, f32[6]{0:T(128)S(1)}, s32[]{:T(128)}, s32[]{:T(128)}) %tuple.64), condition=%wide.region_1.0_spmd, body=%wide.region_0.0_spmd.sunk | while | flops 5621830 | bytes 5973933 | solution.py:75
  18.4 26.3 %collective-permute-done.1 = f32[6,64,1]{2,1,0:T(8,128)S(1)} collective-permute-done((f32[6,64,1]{2,1,0:T(8,128)S(1)}, f32[6,64,1]{2,1,0:T(8,128)S(1)}, u32[]{:S(2)}, u32[]{:S(2)}) %collective-permute-start.1) | collective-permute-done | bytes 1568 | tf_op jit(solution)/shard_map/while/body/eval_jaxpr/ppermute | solution.py:20
  111.4 27.3 %reshape.39 = f32[6,16,4,128,4]{4,3,2,1,0:T(8,128)} reshape(f32[6,64,512]{2,1,0:T(8,128)S(1)} %get-tuple-element.121) | data formatting | bytes 1572864 | tf_op jit(solution)/shard_map/reshape | solution.py:55
  139.2 9.4 %reduce_sum.40 = f32[6,16,128]{2,1,0:T(8,128)S(1)} reduce(f32[6,16,4,128,4]{4,3,2,1,0:T(8,128)} %reshape.39, f32[]{:T(128)} %constant.48.clone.1), dimensions={2,4}, to_apply=%region_2.0 | reduce | flops 184320 | bytes 835588 | tf_op jit(solution)/shard_map/reduce_sum | solution.py:55
  148.6 27.3 %reshape.40 = f32[6,16,4,128,4]{4,3,2,1,0:T(8,128)} reshape(f32[6,64,512]{2,1,0:T(8,128)S(1)} %collective-permute-done.5) | data formatting | bytes 1572864 | tf_op jit(solution)/shard_map/reshape | solution.py:55
  175.9 9.4 %reduce_sum.41 = f32[6,16,128]{2,1,0:T(8,128)S(1)} reduce(f32[6,16,4,128,4]{4,3,2,1,0:T(8,128)} %reshape.40, f32[]{:T(128)} %constant.48.clone.1), dimensions={2,4}, to_apply=%region_3.0 | reduce | flops 184320 | bytes 835588 | tf_op jit(solution)/shard_map/reduce_sum | solution.py:55
  185.4 323.9 %while.25 = (s32[]{:T(128)}, f32[6,16,128]{2,1,0:T(8,128)S(1)}, s32[]{:T(128)}, f32[6,6,16,128]{3,2,1,0:T(8,128)S(1)}, f32[6,16,128]{2,1,0:T(8,128)S(1)}, /*index=5*/s32[]{:T(128)}, s32[]{:T(128)}) while((s32[]{:T(128)}, f32[6,16,128]{2,1,0:T(8,128)S(1)}, s32[]{:T(128)}, f32[6,6,16,128]{3,2,1,0:T(8,128)S(1)}, ...), condition=%wide.region_6.7_spmd.clone, body=%wide.region_4.6_spmd.clone.sunk | while | flops 184324 | bytes 983178 | solution.py:87
  218.3 8.5 %collective-permute-done.4 = f32[6,16,128]{2,1,0:T(8,128)S(1)} collective-permute-done((f32[6,16,128]{2,1,0:T(8,128)S(1)}, f32[6,16,128]{2,1,0:T(8,128)S(1)}, u32[]{:S(2)}, u32[]{:S(2)}) %collective-permute-start.4) | collective-permute-done | bytes 49184 | tf_op jit(solution)/shard_map/while/body/eval_jaxpr/ppermute | solution.py:28
  270.1 8.5 %collective-permute-done.4 = f32[6,16,128]{2,1,0:T(8,128)S(1)} collective-permute-done((f32[6,16,128]{2,1,0:T(8,128)S(1)}, f32[6,16,128]{2,1,0:T(8,128)S(1)}, u32[]{:S(2)}, u32[]{:S(2)}) %collective-permute-start.4) | collective-permute-done | bytes 49184 | tf_op jit(solution)/shard_map/while/body/eval_jaxpr/ppermute | solution.py:28
  290.9 8.3 %collective-permute-done.4 = f32[6,16,128]{2,1,0:T(8,128)S(1)} collective-permute-done((f32[6,16,128]{2,1,0:T(8,128)S(1)}, f32[6,16,128]{2,1,0:T(8,128)S(1)}, u32[]{:S(2)}, u32[]{:S(2)}) %collective-permute-start.4) | collective-permute-done | bytes 49184 | tf_op jit(solution)/shard_map/while/body/eval_jaxpr/ppermute | solution.py:28
  301.3 8.4 %collective-permute-done.4 = f32[6,16,128]{2,1,0:T(8,128)S(1)} collective-permute-done((f32[6,16,128]{2,1,0:T(8,128)S(1)}, f32[6,16,128]{2,1,0:T(8,128)S(1)}, u32[]{:S(2)}, u32[]{:S(2)}) %collective-permute-start.4) | collective-permute-done | bytes 49184 | tf_op jit(solution)/shard_map/while/body/eval_jaxpr/ppermute | solution.py:28
  311.7 8.8 %collective-permute-done.4 = f32[6,16,128]{2,1,0:T(8,128)S(1)} collective-permute-done((f32[6,16,128]{2,1,0:T(8,128)S(1)}, f32[6,16,128]{2,1,0:T(8,128)S(1)}, u32[]{:S(2)}, u32[]{:S(2)}) %collective-permute-start.4) | collective-permute-done | bytes 49184 | tf_op jit(solution)/shard_map/while/body/eval_jaxpr/ppermute | solution.py:28
  322.5 8.3 %collective-permute-done.4 = f32[6,16,128]{2,1,0:T(8,128)S(1)} collective-permute-done((f32[6,16,128]{2,1,0:T(8,128)S(1)}, f32[6,16,128]{2,1,0:T(8,128)S(1)}, u32[]{:S(2)}, u32[]{:S(2)}) %collective-permute-start.4) | collective-permute-done | bytes 49184 | tf_op jit(solution)/shard_map/while/body/eval_jaxpr/ppermute | solution.py:28
  332.8 8.3 %collective-permute-done.4 = f32[6,16,128]{2,1,0:T(8,128)S(1)} collective-permute-done((f32[6,16,128]{2,1,0:T(8,128)S(1)}, f32[6,16,128]{2,1,0:T(8,128)S(1)}, u32[]{:S(2)}, u32[]{:S(2)}) %collective-permute-start.4) | collective-permute-done | bytes 49184 | tf_op jit(solution)/shard_map/while/body/eval_jaxpr/ppermute | solution.py:28
  343.1 8.4 %collective-permute-done.4 = f32[6,16,128]{2,1,0:T(8,128)S(1)} collective-permute-done((f32[6,16,128]{2,1,0:T(8,128)S(1)}, f32[6,16,128]{2,1,0:T(8,128)S(1)}, u32[]{:S(2)}, u32[]{:S(2)}) %collective-permute-start.4) | collective-permute-done | bytes 49184 | tf_op jit(solution)/shard_map/while/body/eval_jaxpr/ppermute | solution.py:28
  353.6 8.5 %collective-permute-done.4 = f32[6,16,128]{2,1,0:T(8,128)S(1)} collective-permute-done((f32[6,16,128]{2,1,0:T(8,128)S(1)}, f32[6,16,128]{2,1,0:T(8,128)S(1)}, u32[]{:S(2)}, u32[]{:S(2)}) %collective-permute-start.4) | collective-permute-done | bytes 49184 | tf_op jit(solution)/shard_map/while/body/eval_jaxpr/ppermute | solution.py:28
  364.2 8.5 %collective-permute-done.4 = f32[6,16,128]{2,1,0:T(8,128)S(1)} collective-permute-done((f32[6,16,128]{2,1,0:T(8,128)S(1)}, f32[6,16,128]{2,1,0:T(8,128)S(1)}, u32[]{:S(2)}, u32[]{:S(2)}) %collective-permute-start.4) | collective-permute-done | bytes 49184 | tf_op jit(solution)/shard_map/while/body/eval_jaxpr/ppermute | solution.py:28
  374.7 8.5 %collective-permute-done.4 = f32[6,16,128]{2,1,0:T(8,128)S(1)} collective-permute-done((f32[6,16,128]{2,1,0:T(8,128)S(1)}, f32[6,16,128]{2,1,0:T(8,128)S(1)}, u32[]{:S(2)}, u32[]{:S(2)}) %collective-permute-start.4) | collective-permute-done | bytes 49184 | tf_op jit(solution)/shard_map/while/body/eval_jaxpr/ppermute | solution.py:28
  385.3 9.1 %collective-permute-done.4 = f32[6,16,128]{2,1,0:T(8,128)S(1)} collective-permute-done((f32[6,16,128]{2,1,0:T(8,128)S(1)}, f32[6,16,128]{2,1,0:T(8,128)S(1)}, u32[]{:S(2)}, u32[]{:S(2)}) %collective-permute-start.4) | collective-permute-done | bytes 49184 | tf_op jit(solution)/shard_map/while/body/eval_jaxpr/ppermute | solution.py:28
  427.4 8.7 %collective-permute-done.4 = f32[6,16,128]{2,1,0:T(8,128)S(1)} collective-permute-done((f32[6,16,128]{2,1,0:T(8,128)S(1)}, f32[6,16,128]{2,1,0:T(8,128)S(1)}, u32[]{:S(2)}, u32[]{:S(2)}) %collective-permute-start.4) | collective-permute-done | bytes 49184 | tf_op jit(solution)/shard_map/while/body/eval_jaxpr/ppermute | solution.py:28
  438.1 8.5 %collective-permute-done.4 = f32[6,16,128]{2,1,0:T(8,128)S(1)} collective-permute-done((f32[6,16,128]{2,1,0:T(8,128)S(1)}, f32[6,16,128]{2,1,0:T(8,128)S(1)}, u32[]{:S(2)}, u32[]{:S(2)}) %collective-permute-start.4) | collective-permute-done | bytes 49184 | tf_op jit(solution)/shard_map/while/body/eval_jaxpr/ppermute | solution.py:28
  448.6 8.5 %collective-permute-done.4 = f32[6,16,128]{2,1,0:T(8,128)S(1)} collective-permute-done((f32[6,16,128]{2,1,0:T(8,128)S(1)}, f32[6,16,128]{2,1,0:T(8,128)S(1)}, u32[]{:S(2)}, u32[]{:S(2)}) %collective-permute-start.4) | collective-permute-done | bytes 49184 | tf_op jit(solution)/shard_map/while/body/eval_jaxpr/ppermute | solution.py:28
  459.2 8.9 %collective-permute-done.4 = f32[6,16,128]{2,1,0:T(8,128)S(1)} collective-permute-done((f32[6,16,128]{2,1,0:T(8,128)S(1)}, f32[6,16,128]{2,1,0:T(8,128)S(1)}, u32[]{:S(2)}, u32[]{:S(2)}) %collective-permute-start.4) | collective-permute-done | bytes 49184 | tf_op jit(solution)/shard_map/while/body/eval_jaxpr/ppermute | solution.py:28
  (248 shorter events, 264.9 us)
Async XLA Ops:
  0.0 148.6 %collective-permute-start.5 = (f32[6,64,512]{2,1,0:T(8,128)}, f32[6,64,512]{2,1,0:T(8,128)S(1)}, u32[]{:S(2)}, u32[]{:S(2)}) collective-permute-start(f32[6,64,512]{2,1,0:T(8,128)} %bitcast.12), channel_id=1, source_target_pairs={{16,0},{32,16},{48,32},{64,48},{80,64},{96,80},{112,96},{128,112},... | collective-permute-start | bytes 2359304 | tf_op jit(solution)/shard_map/ppermute | solution.py:28
  13.3 31.4 %collective-permute-start.1 = (f32[6,64,1]{2,1,0:T(8,128)S(1)}, f32[6,64,1]{2,1,0:T(8,128)S(1)}, u32[]{:S(2)}, u32[]{:S(2)}) collective-permute-start(f32[6,64,1]{2,1,0:T(8,128)S(1)} %get-tuple-element.227), channel_id=1, source_target_pairs={{4,0},{8,4},{12,8},{5,1},{9,5},{13,9},{6,2},{10,6},{14,10},{7,3},{... | collective-permute-start | bytes 4616 | tf_op jit(solution)/shard_map/while/body/eval_jaxpr/ppermute | solution.py:20
  185.5 10.2 %collective-permute-start.4 = (f32[6,16,128]{2,1,0:T(8,128)S(1)}, f32[6,16,128]{2,1,0:T(8,128)S(1)}, u32[]{:S(2)}, u32[]{:S(2)}) collective-permute-start(f32[6,16,128]{2,1,0:T(8,128)S(1)} %add.165), channel_id=1, source_target_pairs={{0,16},{16,32},{32,48},{48,64},{64,80},{80,96},{96,112},{112,128},... | collective-permute-start | bytes 147464 | tf_op jit(solution)/shard_map/while/body/eval_jaxpr/ppermute | solution.py:28
  195.8 10.2 %collective-permute-start.4 = (f32[6,16,128]{2,1,0:T(8,128)S(1)}, f32[6,16,128]{2,1,0:T(8,128)S(1)}, u32[]{:S(2)}, u32[]{:S(2)}) collective-permute-start(f32[6,16,128]{2,1,0:T(8,128)S(1)} %add.165), channel_id=1, source_target_pairs={{0,16},{16,32},{32,48},{48,64},{64,80},{80,96},{96,112},{112,128},... | collective-permute-start | bytes 147464 | tf_op jit(solution)/shard_map/while/body/eval_jaxpr/ppermute | solution.py:28
  206.1 10.2 %collective-permute-start.4 = (f32[6,16,128]{2,1,0:T(8,128)S(1)}, f32[6,16,128]{2,1,0:T(8,128)S(1)}, u32[]{:S(2)}, u32[]{:S(2)}) collective-permute-start(f32[6,16,128]{2,1,0:T(8,128)S(1)} %add.165), channel_id=1, source_target_pairs={{0,16},{16,32},{32,48},{48,64},{64,80},{80,96},{96,112},{112,128},... | collective-permute-start | bytes 147464 | tf_op jit(solution)/shard_map/while/body/eval_jaxpr/ppermute | solution.py:28
  216.4 10.5 %collective-permute-start.4 = (f32[6,16,128]{2,1,0:T(8,128)S(1)}, f32[6,16,128]{2,1,0:T(8,128)S(1)}, u32[]{:S(2)}, u32[]{:S(2)}) collective-permute-start(f32[6,16,128]{2,1,0:T(8,128)S(1)} %add.165), channel_id=1, source_target_pairs={{0,16},{16,32},{32,48},{48,64},{64,80},{80,96},{96,112},{112,128},... | collective-permute-start | bytes 147464 | tf_op jit(solution)/shard_map/while/body/eval_jaxpr/ppermute | solution.py:28
  268.1 10.4 %collective-permute-start.4 = (f32[6,16,128]{2,1,0:T(8,128)S(1)}, f32[6,16,128]{2,1,0:T(8,128)S(1)}, u32[]{:S(2)}, u32[]{:S(2)}) collective-permute-start(f32[6,16,128]{2,1,0:T(8,128)S(1)} %add.165), channel_id=1, source_target_pairs={{0,16},{16,32},{32,48},{48,64},{64,80},{80,96},{96,112},{112,128},... | collective-permute-start | bytes 147464 | tf_op jit(solution)/shard_map/while/body/eval_jaxpr/ppermute | solution.py:28
  278.7 10.2 %collective-permute-start.4 = (f32[6,16,128]{2,1,0:T(8,128)S(1)}, f32[6,16,128]{2,1,0:T(8,128)S(1)}, u32[]{:S(2)}, u32[]{:S(2)}) collective-permute-start(f32[6,16,128]{2,1,0:T(8,128)S(1)} %add.165), channel_id=1, source_target_pairs={{0,16},{16,32},{32,48},{48,64},{64,80},{80,96},{96,112},{112,128},... | collective-permute-start | bytes 147464 | tf_op jit(solution)/shard_map/while/body/eval_jaxpr/ppermute | solution.py:28
  289.0 10.3 %collective-permute-start.4 = (f32[6,16,128]{2,1,0:T(8,128)S(1)}, f32[6,16,128]{2,1,0:T(8,128)S(1)}, u32[]{:S(2)}, u32[]{:S(2)}) collective-permute-start(f32[6,16,128]{2,1,0:T(8,128)S(1)} %add.165), channel_id=1, source_target_pairs={{0,16},{16,32},{32,48},{48,64},{64,80},{80,96},{96,112},{112,128},... | collective-permute-start | bytes 147464 | tf_op jit(solution)/shard_map/while/body/eval_jaxpr/ppermute | solution.py:28
  299.3 10.3 %collective-permute-start.4 = (f32[6,16,128]{2,1,0:T(8,128)S(1)}, f32[6,16,128]{2,1,0:T(8,128)S(1)}, u32[]{:S(2)}, u32[]{:S(2)}) collective-permute-start(f32[6,16,128]{2,1,0:T(8,128)S(1)} %add.165), channel_id=1, source_target_pairs={{0,16},{16,32},{32,48},{48,64},{64,80},{80,96},{96,112},{112,128},... | collective-permute-start | bytes 147464 | tf_op jit(solution)/shard_map/while/body/eval_jaxpr/ppermute | solution.py:28
  309.7 10.7 %collective-permute-start.4 = (f32[6,16,128]{2,1,0:T(8,128)S(1)}, f32[6,16,128]{2,1,0:T(8,128)S(1)}, u32[]{:S(2)}, u32[]{:S(2)}) collective-permute-start(f32[6,16,128]{2,1,0:T(8,128)S(1)} %add.165), channel_id=1, source_target_pairs={{0,16},{16,32},{32,48},{48,64},{64,80},{80,96},{96,112},{112,128},... | collective-permute-start | bytes 147464 | tf_op jit(solution)/shard_map/while/body/eval_jaxpr/ppermute | solution.py:28
  320.6 10.2 %collective-permute-start.4 = (f32[6,16,128]{2,1,0:T(8,128)S(1)}, f32[6,16,128]{2,1,0:T(8,128)S(1)}, u32[]{:S(2)}, u32[]{:S(2)}) collective-permute-start(f32[6,16,128]{2,1,0:T(8,128)S(1)} %add.165), channel_id=1, source_target_pairs={{0,16},{16,32},{32,48},{48,64},{64,80},{80,96},{96,112},{112,128},... | collective-permute-start | bytes 147464 | tf_op jit(solution)/shard_map/while/body/eval_jaxpr/ppermute | solution.py:28
  330.9 10.2 %collective-permute-start.4 = (f32[6,16,128]{2,1,0:T(8,128)S(1)}, f32[6,16,128]{2,1,0:T(8,128)S(1)}, u32[]{:S(2)}, u32[]{:S(2)}) collective-permute-start(f32[6,16,128]{2,1,0:T(8,128)S(1)} %add.165), channel_id=1, source_target_pairs={{0,16},{16,32},{32,48},{48,64},{64,80},{80,96},{96,112},{112,128},... | collective-permute-start | bytes 147464 | tf_op jit(solution)/shard_map/while/body/eval_jaxpr/ppermute | solution.py:28
  341.2 10.4 %collective-permute-start.4 = (f32[6,16,128]{2,1,0:T(8,128)S(1)}, f32[6,16,128]{2,1,0:T(8,128)S(1)}, u32[]{:S(2)}, u32[]{:S(2)}) collective-permute-start(f32[6,16,128]{2,1,0:T(8,128)S(1)} %add.165), channel_id=1, source_target_pairs={{0,16},{16,32},{32,48},{48,64},{64,80},{80,96},{96,112},{112,128},... | collective-permute-start | bytes 147464 | tf_op jit(solution)/shard_map/while/body/eval_jaxpr/ppermute | solution.py:28
  351.6 10.5 %collective-permute-start.4 = (f32[6,16,128]{2,1,0:T(8,128)S(1)}, f32[6,16,128]{2,1,0:T(8,128)S(1)}, u32[]{:S(2)}, u32[]{:S(2)}) collective-permute-start(f32[6,16,128]{2,1,0:T(8,128)S(1)} %add.165), channel_id=1, source_target_pairs={{0,16},{16,32},{32,48},{48,64},{64,80},{80,96},{96,112},{112,128},... | collective-permute-start | bytes 147464 | tf_op jit(solution)/shard_map/while/body/eval_jaxpr/ppermute | solution.py:28
  362.2 10.5 %collective-permute-start.4 = (f32[6,16,128]{2,1,0:T(8,128)S(1)}, f32[6,16,128]{2,1,0:T(8,128)S(1)}, u32[]{:S(2)}, u32[]{:S(2)}) collective-permute-start(f32[6,16,128]{2,1,0:T(8,128)S(1)} %add.165), channel_id=1, source_target_pairs={{0,16},{16,32},{32,48},{48,64},{64,80},{80,96},{96,112},{112,128},... | collective-permute-start | bytes 147464 | tf_op jit(solution)/shard_map/while/body/eval_jaxpr/ppermute | solution.py:28
  372.8 10.5 %collective-permute-start.4 = (f32[6,16,128]{2,1,0:T(8,128)S(1)}, f32[6,16,128]{2,1,0:T(8,128)S(1)}, u32[]{:S(2)}, u32[]{:S(2)}) collective-permute-start(f32[6,16,128]{2,1,0:T(8,128)S(1)} %add.165), channel_id=1, source_target_pairs={{0,16},{16,32},{32,48},{48,64},{64,80},{80,96},{96,112},{112,128},... | collective-permute-start | bytes 147464 | tf_op jit(solution)/shard_map/while/body/eval_jaxpr/ppermute | solution.py:28
  383.3 11.1 %collective-permute-start.4 = (f32[6,16,128]{2,1,0:T(8,128)S(1)}, f32[6,16,128]{2,1,0:T(8,128)S(1)}, u32[]{:S(2)}, u32[]{:S(2)}) collective-permute-start(f32[6,16,128]{2,1,0:T(8,128)S(1)} %add.165), channel_id=1, source_target_pairs={{0,16},{16,32},{32,48},{48,64},{64,80},{80,96},{96,112},{112,128},... | collective-permute-start | bytes 147464 | tf_op jit(solution)/shard_map/while/body/eval_jaxpr/ppermute | solution.py:28
  394.5 10.2 %collective-permute-start.4 = (f32[6,16,128]{2,1,0:T(8,128)S(1)}, f32[6,16,128]{2,1,0:T(8,128)S(1)}, u32[]{:S(2)}, u32[]{:S(2)}) collective-permute-start(f32[6,16,128]{2,1,0:T(8,128)S(1)} %add.165), channel_id=1, source_target_pairs={{0,16},{16,32},{32,48},{48,64},{64,80},{80,96},{96,112},{112,128},... | collective-permute-start | bytes 147464 | tf_op jit(solution)/shard_map/while/body/eval_jaxpr/ppermute | solution.py:28
  404.8 10.2 %collective-permute-start.4 = (f32[6,16,128]{2,1,0:T(8,128)S(1)}, f32[6,16,128]{2,1,0:T(8,128)S(1)}, u32[]{:S(2)}, u32[]{:S(2)}) collective-permute-start(f32[6,16,128]{2,1,0:T(8,128)S(1)} %add.165), channel_id=1, source_target_pairs={{0,16},{16,32},{32,48},{48,64},{64,80},{80,96},{96,112},{112,128},... | collective-permute-start | bytes 147464 | tf_op jit(solution)/shard_map/while/body/eval_jaxpr/ppermute | solution.py:28
  425.4 10.6 %collective-permute-start.4 = (f32[6,16,128]{2,1,0:T(8,128)S(1)}, f32[6,16,128]{2,1,0:T(8,128)S(1)}, u32[]{:S(2)}, u32[]{:S(2)}) collective-permute-start(f32[6,16,128]{2,1,0:T(8,128)S(1)} %add.165), channel_id=1, source_target_pairs={{0,16},{16,32},{32,48},{48,64},{64,80},{80,96},{96,112},{112,128},... | collective-permute-start | bytes 147464 | tf_op jit(solution)/shard_map/while/body/eval_jaxpr/ppermute | solution.py:28
  436.1 10.5 %collective-permute-start.4 = (f32[6,16,128]{2,1,0:T(8,128)S(1)}, f32[6,16,128]{2,1,0:T(8,128)S(1)}, u32[]{:S(2)}, u32[]{:S(2)}) collective-permute-start(f32[6,16,128]{2,1,0:T(8,128)S(1)} %add.165), channel_id=1, source_target_pairs={{0,16},{16,32},{32,48},{48,64},{64,80},{80,96},{96,112},{112,128},... | collective-permute-start | bytes 147464 | tf_op jit(solution)/shard_map/while/body/eval_jaxpr/ppermute | solution.py:28
  446.7 10.5 %collective-permute-start.4 = (f32[6,16,128]{2,1,0:T(8,128)S(1)}, f32[6,16,128]{2,1,0:T(8,128)S(1)}, u32[]{:S(2)}, u32[]{:S(2)}) collective-permute-start(f32[6,16,128]{2,1,0:T(8,128)S(1)} %add.165), channel_id=1, source_target_pairs={{0,16},{16,32},{32,48},{48,64},{64,80},{80,96},{96,112},{112,128},... | collective-permute-start | bytes 147464 | tf_op jit(solution)/shard_map/while/body/eval_jaxpr/ppermute | solution.py:28
  457.2 10.9 %collective-permute-start.4 = (f32[6,16,128]{2,1,0:T(8,128)S(1)}, f32[6,16,128]{2,1,0:T(8,128)S(1)}, u32[]{:S(2)}, u32[]{:S(2)}) collective-permute-start(f32[6,16,128]{2,1,0:T(8,128)S(1)} %add.165), channel_id=1, source_target_pairs={{0,16},{16,32},{32,48},{48,64},{64,80},{80,96},{96,112},{112,128},... | collective-permute-start | bytes 147464 | tf_op jit(solution)/shard_map/while/body/eval_jaxpr/ppermute | solution.py:28
  (26 other events, 200.9 us)
where the time goes:
time: 516 us; the launch traced here: 514 us
  waiting for transfers between devices  315 us (61%)
  starting transfers between devices  109 us (21%)
  local copies, waits for them, and re-layouts  60.3 us (12%)
  other arithmetic  27.2 us (5%)
    ppermute x32, waiting for transfers between devices, passed_along(): lax.ppermute(value, axis, [(source, source + steps) for source in range(i...  261 us
    ppermute x32, starting transfers between devices, passed_along(): lax.ppermute(value, axis, [(source, source + steps) for source in range(i...  69.6 us
    reshape x2, local copies, waits for them, and re-layouts, restrict(): field.reshape(count, height_rows // 4, 4, width_cols // 4, 4)  54.7 us
    ppermute x8, waiting for transfers between devices, extended_2(): after = lax.ppermute(initial, axis, down)  48.4 us
    ppermute x8, starting transfers between devices, extended_2(): after = lax.ppermute(initial, axis, down)  19.7 us
    ppermute x8, starting transfers between devices, extended_2(): before = lax.ppermute(last, axis, up)  19.5 us
    reduce_sum x2, other arithmetic, restrict(): field.reshape(count, height_rows // 4, 4, width_cols // 4, 4)  18.8 us
  transfers between devices with their start and end apart: 48, of which 47 were waited for; matrix products, arithmetic and copies ran while one was open for 9% of the time, Pallas kernels for 0%

commit v1 on v0

v1 whole, which is shorter than its diff:
```python
import functools

import jax
import jax.numpy as jnp
from jax import lax
from jax.experimental import pallas as pl
from jax.experimental.pallas import tpu as pltpu
from jax.sharding import PartitionSpec as P

FSTEPS = 4
STEP = 0.24
FACE = 0.24 * 0.25 * 0.25
F32 = jnp.float32
TOP = 16
BUF = 96
PARAMS = pltpu.CompilerParams(vmem_limit_bytes=24 << 20)
VMEM = pl.BlockSpec(memory_space=pltpu.VMEM)
SMEM = pl.BlockSpec(memory_space=pltpu.SMEM)


def lanes(shape):
    return lax.broadcasted_iota(jnp.int32, shape, len(shape) - 1)


def columns_kernel(first_ref, last_ref, above0_ref, above3_ref, below0_ref, below3_ref, right_ref, left_ref):
    def packed(refs, shift):
        for rows, ref in refs:
            lane = lanes(ref.shape[1:])
            total = jnp.zeros(ref.shape[1:], F32)
            for f in range(6):
                moved = pltpu.roll(ref[f], (4 * f + shift) % 128, 1)
                total = jnp.where((lane >= 4 * f) & (lane < 4 * f + 4), moved, total)
            yield rows, total

    for rows, total in packed(((0, last_ref), (64, below3_ref), (68, above3_ref)), 4):
        right_ref[rows : rows + total.shape[0], :] = total
    for rows, total in packed(((0, first_ref), (64, below0_ref), (68, above0_ref)), 0):
        left_ref[rows : rows + total.shape[0], :] = total


def pack_columns(state, above, below):
    whole = lambda t: pl.BlockSpec((6, 64, 128), lambda i: (0, 0, t))
    strip = lambda t: pl.BlockSpec((6, 4, 128), lambda i: (0, 0, t))
    out = jax.ShapeDtypeStruct((72, 128), F32)
    spec = pl.BlockSpec((72, 128), lambda i: (0, 0))
    return pl.pallas_call(
        columns_kernel,
        grid=(1,),
        out_shape=(out, out),
        in_specs=[whole(0), whole(3), strip(0), strip(3), strip(0), strip(3)],
        out_specs=(spec, spec),
        compiler_params=PARAMS,
        name="columns",
    )(state, state, above, above, below, below)


def restricted(buffer, slot, sums):
    for f in range(6):
        for t in range(4):
            total = buffer[slot, f, t, pl.ds(TOP, 16, stride=4), :]
            for k in range(1, 4):
                total = total + buffer[slot, f, t, pl.ds(TOP + k, 16, stride=4), :]
            sums[16 * f : 16 * f + 16, 128 * t : 128 * t + 128] = total
    cell = lax.broadcasted_iota(jnp.int32, (512, 128), 0)
    coarse = lax.broadcasted_iota(jnp.int32, (512, 128), 1)
    average = jnp.where(cell // 4 == coarse, F32(1.0 / 16.0), F32(0.0))
    return jnp.dot(sums[...], average, precision=lax.Precision.HIGHEST, preferred_element_type=F32)


def put_pair(packed_ref, k, low, high):
    left = lanes(low.shape) < 64
    even = jnp.where(left, low, pltpu.roll(high, 64, 1))
    odd = jnp.where(left, pltpu.roll(low, 64, 1), high)
    packed_ref[pl.ds(k, 16, stride=48), :] = even
    packed_ref[pl.ds(24 + k, 16, stride=48), :] = odd


def fine_kernel(place_ref, nu_ref, state_ref, above_ref, below_ref, from_left_ref, from_right_ref, map_ref,
                fine_ref, packed_ref, buffer, face, weights, sums):
    row, column = place_ref[0], place_ref[1]
    lane = lanes((8, 128))
    for f in range(6):
        for t in range(4):
            cut = slice(128 * t, 128 * t + 128)
            buffer[0, f, t, TOP : TOP + 64, :] = state_ref[f, :, cut]
            buffer[0, f, t, TOP - 4 : TOP, :] = above_ref[f, :, cut]
            buffer[0, f, t, TOP + 64 : TOP + 68, :] = below_ref[f, :, cut]
        for source, target, count in ((0, TOP, 64), (64, TOP + 64, 4), (68, TOP - 4, 4)):
            at = lanes((count, 128))
            right = pltpu.roll(from_right_ref[source : source + count, :], (128 - 4 * f) % 128, 1)
            left = pltpu.roll(from_left_ref[source : source + count, :], 124 - 4 * f, 1)
            halo = jnp.where(at < 4, right, jnp.where(at >= 124, left, F32(0.0)))
            buffer[0, f, 4, target : target + count, :] = halo
    cell = lax.broadcasted_iota(jnp.int32, (BUF, 128), 0) - TOP + row * 64
    radius = cell.astype(F32)
    weights[0] = (radius + 1.0) / (radius + 0.5)
    weights[1] = radius / (radius + 0.5)
    for f in range(6):
        for j in range(3):
            put_pair(packed_ref, 3 * f + j, map_ref[6 * f + j], map_ref[6 * f + j + 3])
    means = restricted(buffer, 0, sums)
    for j in range(3):
        put_pair(packed_ref, 21 + j, means[16 * j : 16 * j + 16], means[16 * j + 48 : 16 * j + 64])

    low, high = jnp.where(column < 3, 64, 0), jnp.where(column > 0, 64, 128)
    inside_side = (lane < low) | (lane >= high)

    def east(values):
        moved = [pltpu.roll(v, 127, 1) for v in values]
        n = len(moved)
        return [jnp.where(lane < 127, moved[t], moved[(t + 1) % n]) for t in range(n)]

    def west(values):
        moved = [pltpu.roll(v, 1, 1) for v in values]
        n = len(moved)
        return [jnp.where(lane > 0, moved[t], moved[(t - 1) % n]) for t in range(n)]

    def one_step(step, last):
        now, later = step % 2, (step + 1) % 2
        tiles = range(2, 10) if last else range(1, 11)
        for i in tiles:
            rows = pl.ds(8 * i, 8)
            speed = [FACE * jnp.tanh(buffer[now, 1, t, rows, :]) for t in range(5)]
            for t, (a, b) in enumerate(zip(speed, east(speed))):
                face[t, rows, :] = a + b

        def one_field(f, nothing):
            k = STEP * nu_ref[f]
            keep = 1.0 - 2.0 * k
            for i in tiles:
                rows = pl.ds(8 * i, 8)
                center = [buffer[now, f, t, rows, :] for t in range(5)]
                flux = []
                for t, (c, e) in enumerate(zip(center, east(center))):
                    g = face[t, rows, :]
                    flux.append(e * (k - g) - c * (k + g))
                back = west(flux)
                up, down = weights[0, rows, :], weights[1, rows, :]
                for t in range(4 if last else 5):
                    north = buffer[now, f, t, pl.ds(8 * i + 1, 8), :]
                    south = buffer[now, f, t, pl.ds(8 * i - 1, 8), :]
                    new = keep * center[t] + k * (up * north + down * south) + (flux[t] - back[t])
                    if i == 1:
                        new = jnp.where(row > 0, new, F32(0.0))
                    if i == 10:
                        new = jnp.where(row < 3, new, F32(0.0))
                    if t == 4:
                        new = jnp.where(inside_side, new, F32(0.0))
                    buffer[later, f, t, rows, :] = new
                    if last:
                        fine_ref[f, 8 * i - TOP : 8 * i - TOP + 8, 128 * t : 128 * t + 128] = new
            return nothing

        lax.fori_loop(0, 6, one_field, 0)

    for step in range(FSTEPS):
        one_step(step, step == FSTEPS - 1)
    means = restricted(buffer, FSTEPS % 2, sums)
    for j in range(3):
        put_pair(packed_ref, 18 + j, means[16 * j : 16 * j + 16], means[16 * j + 48 : 16 * j + 64])


def fine(place, diffusivity, state, above, below, from_left, from_right, coarse_map):
    return pl.pallas_call(
        fine_kernel,
        out_shape=(jax.ShapeDtypeStruct((6, 64, 512), F32), jax.ShapeDtypeStruct((768, 128), F32)),
        in_specs=[SMEM, SMEM] + [VMEM] * 6,
        out_specs=(VMEM, VMEM),
        scratch_shapes=[
            pltpu.VMEM((2, 6, 5, BUF, 128), F32),
            pltpu.VMEM((5, BUF, 128), F32),
            pltpu.VMEM((2, BUF, 128), F32),
            pltpu.VMEM((96, 512), F32),
        ],
        compiler_params=PARAMS,
        name="fine",
    )(place, diffusivity, state, above, below, from_left, from_right, coarse_map)


def scan_kernel(slices, packed_ref, mapped_ref):
    left = lanes((1, 128)) < 64
    carry = [jnp.zeros((1, 128), F32)] * 3
    for n in range(slices):
        base = 24 * n
        line = lambda k: packed_ref[pl.ds(base + k, 1), :]
        sums = []
        for f in range(6):
            sums.append(line(3 * f) * carry[0] + line(3 * f + 1) * carry[1] + line(3 * f + 2) * carry[2])
        mapped = []
        for j in range(3):
            own = jnp.where(left, sums[j], sums[j + 3])
            other = jnp.where(left, sums[j + 3], sums[j])
            mapped.append(own + pltpu.roll(other, 64, 1))
            mapped_ref[pl.ds(4 * n + j, 1), :] = mapped[j]
        if n < slices - 1:
            carry = [
                mapped[j] + (line(18 + j) - packed_ref[pl.ds(base + 24 + 21 + j, 1), :]) for j in range(3)
            ]


def scanned(packed, slices):
    return pl.pallas_call(
        functools.partial(scan_kernel, slices),
        out_shape=jax.ShapeDtypeStruct((4 * slices, 128), F32),
        in_specs=[VMEM],
        out_specs=VMEM,
        compiler_params=PARAMS,
        name="scan",
    )(packed)


def final_kernel(fine_ref, mapped_ref, out_ref, wide):
    left = lanes((16, 128)) < 64
    upper = lax.broadcasted_iota(jnp.int32, (8, 128), 0) < 4
    for f in range(6):
        j = f % 3
        even = mapped_ref[pl.ds(j, 16, stride=8), :]
        odd = mapped_ref[pl.ds(4 + j, 16, stride=8), :]
        if f < 3:
            cells = jnp.where(left, even, pltpu.roll(odd, 64, 1))
        else:
            cells = jnp.where(left, pltpu.roll(even, 64, 1), odd)
        for t in range(4):
            source = 32 * t + lanes((16, 128)) // 4
            wide[f, t] = jnp.take_along_axis(cells, source, axis=1)
    for f in range(6):
        for t in range(4):
            cut = slice(128 * t, 128 * t + 128)
            for q in range(8):
                first = jnp.broadcast_to(wide[f, t, pl.ds(2 * q, 1), :], (8, 128))
                second = jnp.broadcast_to(wide[f, t, pl.ds(2 * q + 1, 1), :], (8, 128))
                rows = slice(8 * q, 8 * q + 8)
                out_ref[f, rows, cut] = fine_ref[f, rows, cut] + jnp.where(upper, first, second)


def final(fine_state, mapped):
    return pl.pallas_call(
        final_kernel,
        out_shape=jax.ShapeDtypeStruct((6, 64, 512), F32),
        in_specs=[VMEM, VMEM],
        out_specs=VMEM,
        scratch_shapes=[pltpu.VMEM((6, 4, 16, 128), F32)],
        compiler_params=PARAMS,
        name="final",
    )(fine_state, mapped)


def swapped(first, last, axis):
    size = lax.axis_size(axis)
    up = [(i, i + 1) for i in range(size - 1)]
    down = [(i + 1, i) for i in range(size - 1)]
    return lax.ppermute(last, axis, up), lax.ppermute(first, axis, down)


def local(starts, coarse_map, diffusivity):
    state, entries = starts[0], coarse_map[0]
    slices = lax.axis_size("tm")
    place = jnp.stack([lax.axis_index("row"), lax.axis_index("gz")]).astype(jnp.int32)
    above, below = swapped(state[:, :4, :], state[:, 60:, :], "row")
    to_right, to_left = pack_columns(state, above, below)
    from_left, from_right = swapped(to_left, to_right, "gz")
    fine_state, packed = fine(place, diffusivity, state, above, below, from_left, from_right, entries)
    packed = lax.all_to_all(packed, "tm", 0, 0, tiled=True)
    mapped = scanned(packed, slices)
    mapped = lax.all_to_all(mapped, "tm", 0, 0, tiled=True)
    return final(fine_state, mapped)[None]


def solution(mesh):
    placed = (P("tm", None, "row", "gz"), P("tm", None, "row", "gz"), P())
    return jax.shard_map(
        local, mesh=mesh, in_specs=placed, out_specs=P("tm", None, "row", "gz"), check_vma=False
    )
```

time: 516 us -> 77.8 us (0.15)
  the two profiles are of different devices: /device:TPU:96 before, /device:TPU:6 now
where the time goes in v1:
time: 77.8 us; the launch traced here: 77.5 us
  blocking collectives  49.3 us (63%)
  Pallas kernels  10.3 us (13%)
  waiting for transfers between devices  9.01 us (12%)
  starting transfers between devices  6.61 us (8%)
  local copies, waits for them, and re-layouts  2.1 us (3%)
    all_to_all x1, blocking collectives, local(): packed = lax.all_to_all(packed, 'tm', 0, 0, tiled=True)  30.6 us
    all_to_all x1, blocking collectives, local(): mapped = lax.all_to_all(mapped, 'tm', 0, 0, tiled=True)  18.7 us
    ppermute x4, waiting for transfers between devices, swapped(): return (lax.ppermute(last, axis, up), lax.ppermute(first, axis, down))  9.01 us
    ppermute x4, starting transfers between devices, swapped(): return (lax.ppermute(last, axis, up), lax.ppermute(first, axis, down))  6.61 us
    pallas_call x1, Pallas kernels, fine(): pl.pallas_call(fine_kernel, out_shape=(jax.ShapeDtypeStruct((6, 64, 512),...  6.6 us
    pallas_call x1, Pallas kernels, scanned(): pl.pallas_call(functools.partial(scan_kernel, slices), out_shape=jax.Shap...  2.35 us
  transfers between devices with their start and end apart: 4, of which 3 were waited for; matrix products, arithmetic and copies ran while one was open for 0% of the time, Pallas kernels for 0%

profile of v1, /device:TPU:6, one launch (start us, length us, event | category | flops | bytes accessed | tf_op | source)
XLA Modules:
  0.0 77.5 jit_solution(167216099251281008)
XLA Ops:
  0.0 1.0 %fusion = (f32[6,4,512]{2,1,0:T(4,128)S(1)}, f32[6,4,512]{2,1,0:T(4,128)S(1)}) fusion(f32[6,64,512]{2,1,0:T(8,128)} %bitcast.9), kind=kLoop, calls=%fused_computation.1 | loop fusion | bytes 196608 | tf_op jit(solution)/shard_map/slice | solution.py:259
  1.0 2.7 %collective-permute-start.1 = (f32[6,4,512]{2,1,0:T(4,128)S(1)}, f32[6,4,512]{2,1,0:T(4,128)S(1)}, u32[]{:S(2)}, u32[]{:S(2)}) collective-permute-start(f32[6,4,512]{2,1,0:T(4,128)S(1)} %get-tuple-element.13), channel_id=1, source_target_pairs={{1,0},{2,1},{3,2},{5,4},{6,5},{7,6},{9,8},{10,9},{11,10},{13,12},{... | collective-permute-start | bytes 147464 | tf_op jit(solution)/shard_map/ppermute | solution.py:252
  3.7 1.3 %collective-permute-start = (f32[6,4,512]{2,1,0:T(4,128)S(1)}, f32[6,4,512]{2,1,0:T(4,128)S(1)}, u32[]{:S(2)}, u32[]{:S(2)}) collective-permute-start(f32[6,4,512]{2,1,0:T(4,128)S(1)} %get-tuple-element.14), channel_id=1, source_target_pairs={{0,1},{1,2},{2,3},{4,5},{5,6},{6,7},{8,9},{9,10},{10,11},{12,13},{... | collective-permute-start | bytes 147464 | tf_op jit(solution)/shard_map/ppermute | solution.py:252
  5.0 0.4 collective-permute-done.1.below0_ref.below3_ref.below_ref
  5.4 4.3 %collective-permute-done.above0_ref.above3_ref.above_ref = f32[6,4,512]{2,1,0:T(4,128)S(1)} collective-permute-done((f32[6,4,512]{2,1,0:T(4,128)S(1)}, f32[6,4,512]{2,1,0:T(4,128)S(1)}, u32[]{:S(2)}, u32[]{:S(2)}) %collective-permute-start) | collective-permute-done | bytes 49184 | tf_op jit(solution)/shard_map/ppermute | solution.py:252
  9.7 0.0 copy-start
  9.7 1.1 %copy-done = f32[1,6,64,512]{3,2,1,0:T(8,128)S(1)} copy-done((f32[1,6,64,512]{3,2,1,0:T(8,128)S(1)}, f32[1,6,64,512]{3,2,1,0:T(8,128)}, u32[]{:S(2)}) %copy-start) | copy-done | bytes 786456
  10.8 0.0 copy-start.1
  10.8 0.2 columns.1
  11.0 1.3 %collective-permute-start.2 = (f32[72,128]{1,0:T(8,128)S(1)}, f32[72,128]{1,0:T(8,128)S(1)}, u32[]{:S(2)}, u32[]{:S(2)}) collective-permute-start(f32[72,128]{1,0:T(8,128)S(1)} %get-tuple-element.9), channel_id=1, source_target_pairs={{0,4},{4,8},{8,12},{1,5},{5,9},{9,13},{2,6},{6,10},{10,14},{3,7},{... | collective-permute-start | bytes 110600 | tf_op jit(solution)/shard_map/ppermute | solution.py:252
  12.3 1.3 %collective-permute-start.3 = (f32[72,128]{1,0:T(8,128)S(1)}, f32[72,128]{1,0:T(8,128)S(1)}, u32[]{:S(2)}, u32[]{:S(2)}) collective-permute-start(f32[72,128]{1,0:T(8,128)S(1)} %get-tuple-element.10), channel_id=1, source_target_pairs={{4,0},{8,4},{12,8},{5,1},{9,5},{13,9},{6,2},{10,6},{14,10},{7,3},{... | collective-permute-start | bytes 110600 | tf_op jit(solution)/shard_map/ppermute | solution.py:252
  13.6 0.1 pad_add_fusion.place_ref
  13.7 0.0 copy-start.2
  13.7 0.0 collective-permute-done.2.from_left_ref
  13.7 4.3 %collective-permute-done.3.from_right_ref = f32[72,128]{1,0:T(8,128)S(1)} collective-permute-done((f32[72,128]{1,0:T(8,128)S(1)}, f32[72,128]{1,0:T(8,128)S(1)}, u32[]{:S(2)}, u32[]{:S(2)}) %collective-permute-start.3) | collective-permute-done | bytes 36896 | tf_op jit(solution)/shard_map/ppermute | solution.py:252
  18.0 0.0 copy-done.1
  18.0 0.0 copy-done.2
  18.0 6.6 %fine.1 = (f32[6,64,512]{2,1,0:T(8,128)S(1)}, f32[768,128]{1,0:T(8,128)S(1)}) custom-call(s32[2]{0:T(128)S(1)} %pad_add_fusion.place_ref, f32[6]{0:T(128)S(1)} %copy-done.2, f32[6,64,512]{2,1,0:T(8,128)S(1)} %bitcast.12, f32[6,4,512]{2,1,0:T(4,128)S(1)} %collective-permute-done.above0_ref.above3_ref.above_ref, ...), custom_call_target="tpu_custom_call" | custom-call | tf_op jit(solution)/shard_map/fine/pallas_call | solution.py:164
  24.6 30.6 %all_to_all.22 = f32[32,24,128]{2,1,0:T(8,128)S(1)} all-to-all(f32[32,24,128]{2,1,0:T(8,128)S(1)} %bitcast.14), channel_id=1, replica_groups=mesh['tm'=32,'gz'=4,'row'=4] {'tm'}, dimensions={0} | all-to-all | bytes 786432 | tf_op jit(solution)/shard_map/all_to_all | solution.py:263
  55.3 2.3 %scan.1 = f32[128,128]{1,0:T(8,128)S(1)} custom-call(f32[768,128]{1,0:T(8,128)S(1)} %bitcast.13), custom_call_target="tpu_custom_call" | custom-call | tf_op jit(solution)/shard_map/scan/pallas_call | solution.py:202
  57.6 18.7 %all_to_all.23 = f32[32,4,128]{2,1,0:T(4,128)S(1)} all-to-all(f32[32,4,128]{2,1,0:T(4,128)S(1)} %bitcast.17), channel_id=1, replica_groups=mesh['tm'=32,'gz'=4,'row'=4] {'tm'}, dimensions={0} | all-to-all | bytes 131072 | tf_op jit(solution)/shard_map/all_to_all | solution.py:265
  76.3 1.2 %final.1 = f32[6,64,512]{2,1,0:T(8,128)} custom-call(f32[6,64,512]{2,1,0:T(8,128)S(1)} %get-tuple-element.11.fine_ref, f32[128,128]{1,0:T(8,128)S(1)} %bitcast.16), custom_call_target="tpu_custom_call" | custom-call | tf_op jit(solution)/shard_map/final/pallas_call | solution.py:237
Async XLA Ops:
  1.0 4.5 %collective-permute-start.1 = (f32[6,4,512]{2,1,0:T(4,128)S(1)}, f32[6,4,512]{2,1,0:T(4,128)S(1)}, u32[]{:S(2)}, u32[]{:S(2)}) collective-permute-start(f32[6,4,512]{2,1,0:T(4,128)S(1)} %get-tuple-element.13), channel_id=1, source_target_pairs={{1,0},{2,1},{3,2},{5,4},{6,5},{7,6},{9,8},{10,9},{11,10},{13,12},{... | collective-permute-start | bytes 147464 | tf_op jit(solution)/shard_map/ppermute | solution.py:252
  3.7 6.0 %collective-permute-start = (f32[6,4,512]{2,1,0:T(4,128)S(1)}, f32[6,4,512]{2,1,0:T(4,128)S(1)}, u32[]{:S(2)}, u32[]{:S(2)}) collective-permute-start(f32[6,4,512]{2,1,0:T(4,128)S(1)} %get-tuple-element.14), channel_id=1, source_target_pairs={{0,1},{1,2},{2,3},{4,5},{5,6},{6,7},{8,9},{9,10},{10,11},{12,13},{... | collective-permute-start | bytes 147464 | tf_op jit(solution)/shard_map/ppermute | solution.py:252
  9.7 1.1 %copy-start = (f32[1,6,64,512]{3,2,1,0:T(8,128)S(1)}, f32[1,6,64,512]{3,2,1,0:T(8,128)}, u32[]{:S(2)}) copy-start(f32[1,6,64,512]{3,2,1,0:T(8,128)} %param.3) | copy-start | bytes 2359300
  10.8 7.2 %copy-start.1 = (f32[1,36,16,128]{3,2,1,0:T(8,128)S(1)}, f32[1,36,16,128]{3,2,1,0:T(8,128)}, u32[]{:S(2)}) copy-start(f32[1,36,16,128]{3,2,1,0:T(8,128)} %param.4) | copy-start | bytes 884740
  11.0 2.7 %collective-permute-start.2 = (f32[72,128]{1,0:T(8,128)S(1)}, f32[72,128]{1,0:T(8,128)S(1)}, u32[]{:S(2)}, u32[]{:S(2)}) collective-permute-start(f32[72,128]{1,0:T(8,128)S(1)} %get-tuple-element.9), channel_id=1, source_target_pairs={{0,4},{4,8},{8,12},{1,5},{5,9},{9,13},{2,6},{6,10},{10,14},{3,7},{... | collective-permute-start | bytes 110600 | tf_op jit(solution)/shard_map/ppermute | solution.py:252
  12.3 5.7 %collective-permute-start.3 = (f32[72,128]{1,0:T(8,128)S(1)}, f32[72,128]{1,0:T(8,128)S(1)}, u32[]{:S(2)}, u32[]{:S(2)}) collective-permute-start(f32[72,128]{1,0:T(8,128)S(1)} %get-tuple-element.10), channel_id=1, source_target_pairs={{4,0},{8,4},{12,8},{5,1},{9,5},{13,9},{6,2},{10,6},{14,10},{7,3},{... | collective-permute-start | bytes 110600 | tf_op jit(solution)/shard_map/ppermute | solution.py:252
  13.7 4.3 %copy-start.2 = (f32[6]{0:T(128)S(1)}, f32[6]{0:T(128)}, u32[]{:S(2)}) copy-start(f32[6]{0:T(128)} %nu_ref.1) | copy-start | bytes 76

commit v2 on v0

v2 whole, which is shorter than its diff:
```python
import functools

import jax
import jax.numpy as jnp
from jax import lax
from jax.experimental import pallas as pl
from jax.experimental.pallas import tpu as pltpu
from jax.sharding import PartitionSpec as P

FSTEPS = 4
STEP = 0.24
FACE = 0.24 * 0.25 * 0.25
F32, BF16 = jnp.float32, jnp.bfloat16
TOP = 16
BUF = 96
PARAMS = pltpu.CompilerParams(vmem_limit_bytes=24 << 20)
VMEM = pl.BlockSpec(memory_space=pltpu.VMEM)
SMEM = pl.BlockSpec(memory_space=pltpu.SMEM)
HBM = pl.BlockSpec(memory_space=pltpu.HBM)


def lanes(shape):
    return lax.broadcasted_iota(jnp.int32, shape, len(shape) - 1)


def put_pair(packed_ref, k, low, high):
    left = lanes(low.shape) < 64
    packed_ref[pl.ds(k, 16, stride=48), :] = jnp.where(left, low, pltpu.roll(high, 64, 1))
    packed_ref[pl.ds(24 + k, 16, stride=48), :] = jnp.where(left, pltpu.roll(low, 64, 1), high)


def split_dot(x, matrix, transposed=False):
    high = x.astype(BF16)
    low = (x - high.astype(F32)).astype(BF16)
    dims = (((1,), (1 if transposed else 0,)), ((), ()))
    dot = lambda part: lax.dot_general(part, matrix, dims, preferred_element_type=F32)
    return dot(high) + dot(low)


PLACES = [(0, q, q) for q in range(4)] + [(1, q, 4 + q) for q in range(2)] + [(2, q, 1) for q in range(4)]


def moved(x, shift):
    shift = shift % 128
    return pltpu.roll(x, shift, 1) if shift else x


def messages(column, count):
    lane = lanes((count, 128))
    right, left = jnp.zeros((count, 128), F32), jnp.zeros((count, 128), F32)
    for tile, q, f in PLACES:
        at = 32 * q + 4 * tile
        right = jnp.where((lane >= at) & (lane < at + 4), moved(column(f, 3), at + 4), right)
        at = 32 * q + 24 - 4 * tile
        left = jnp.where((lane >= at) & (lane < at + 4), moved(column(f, 0), at), left)
    return right, left


def put_strips(strips_ref, rows, column, count):
    lane = lanes((count, 128))
    for tile in range(3):
        total = jnp.zeros((count, 128), F32)
        for other, q, f in PLACES:
            if other == tile:
                at = 32 * q
                total = jnp.where((lane >= at + 4) & (lane < at + 12), moved(column(f, 0), at + 4), total)
                total = jnp.where((lane >= at + 16) & (lane < at + 24), moved(column(f, 3), at + 24), total)
        strips_ref[tile, rows : rows + count, :] = total


def prep_kernel(place_ref, nu_ref, starts_ref, map_ref, cells_ref, packed_ref, pair_ref, cross_ref, strips_ref,
                consts_ref, weights_ref, order_ref, spread_ref, state, entries, sems):
    row, column = place_ref[0], place_ref[1]
    state_copy = pltpu.make_async_copy(starts_ref, state, sems.at[0])
    map_copy = pltpu.make_async_copy(map_ref, entries, sems.at[1])
    state_copy.start()
    map_copy.start()
    for t in range(4):
        z = lax.broadcasted_iota(jnp.int32, (128, 512), 0) + 128 * t
        place = lax.broadcasted_iota(jnp.int32, (128, 512), 1)
        order_ref[128 * t : 128 * t + 128, :] = jnp.where(128 * (z % 4) + z // 4 == place, F32(1), F32(0)).astype(BF16)
    lane = lax.broadcasted_iota(jnp.int32, (256, 384), 0)
    target = lax.broadcasted_iota(jnp.int32, (256, 384), 1)
    field, at = lane // 32, lane % 32
    base = jnp.where(field < 3, 128 * field, 128 * (field - 3) + 64)
    to = jnp.where((at >= 4) & (at < 8), base, jnp.where((at >= 20) & (at < 24), base + 63, -1))
    to = jnp.where(field < 6, to, -1)
    spread_ref[...] = jnp.where(to == target, F32(1.0 / 16.0), F32(0.0)).astype(BF16)
    line, lane = lax.broadcasted_iota(jnp.int32, (8, 128), 0), lanes((8, 128))
    flag = lambda condition: jnp.where(condition, F32(1.0), F32(0.0))
    group, at = lane // 32, lane % 32
    low, high = jnp.where(column > 0, 0, 4), jnp.where(column < 3, 32, 24)
    rates = lambda fields: functools.reduce(
        lambda a, q: jnp.where(group == q, STEP * nu_ref[fields[q]], a), range(4), jnp.zeros((8, 128), F32)
    )
    values = [flag(row % 2 == 1), flag(column % 2 == 1), flag(row > 0), flag(row < 3)]
    values += [flag((at >= low) & (at < high)), rates((0, 1, 2, 3)), rates((4, 5, 5, 5)), rates((1, 1, 1, 1))]
    total = jnp.zeros((8, 128), F32)
    for r, value in enumerate(values):
        total = jnp.where(line == r, value, total)
    consts_ref[...] = total
    radius = (lax.broadcasted_iota(jnp.int32, (BUF, 128), 0) - TOP + row * 64).astype(F32)
    weights_ref[0] = (radius + 1.0) / (radius + 0.5)
    weights_ref[1] = radius / (radius + 0.5)

    state_copy.wait()
    piece = lambda f, t: state[f, :, 128 * t : 128 * t + 128]
    odd = column % 2 == 1
    right, left = messages(piece, 64)
    pair_ref[0:64, :] = jnp.where(odd, left, right)
    cross_ref[0:64, :] = jnp.where(odd, right, left)
    put_strips(strips_ref, 0, piece, 64)
    ordered = split_dot(state[...].reshape(384, 512), order_ref[...])
    for f in range(6):
        for k in range(4):
            cells_ref[f, k] = ordered[64 * f : 64 * f + 64, 128 * k : 128 * k + 128]
    put_means(packed_ref, 21, lambda f, k, r: cells_ref[f, k, pl.ds(r, 16, stride=4), :], False)
    map_copy.wait()
    for f in range(6):
        for j in range(3):
            put_pair(packed_ref, 3 * f + j, entries[6 * f + j], entries[6 * f + j + 3])


def put_means(packed_ref, at, load, inner):
    means = []
    for f in range(6):
        total = jnp.zeros((16, 128), F32)
        for k in range(4):
            total = total + ((load(f, k, 0) + load(f, k, 1)) + (load(f, k, 2) + load(f, k, 3)))
        if inner:
            lane = lanes((16, 128))
            total = jnp.where((lane > 0) & (lane < 127), total, F32(0.0))
        means.append(total * F32(1.0 / 16.0))
    for j in range(3):
        put_pair(packed_ref, at + j, means[j], means[j + 3])


def prep(place, diffusivity, state, coarse_map):
    shape = lambda *dims: jax.ShapeDtypeStruct(dims, F32)
    return pl.pallas_call(
        prep_kernel,
        out_shape=(
            shape(6, 4, 64, 128),
            shape(768, 128),
            shape(72, 128),
            shape(72, 128),
            shape(3, 72, 128),
            shape(8, 128),
            shape(2, BUF, 128),
            jax.ShapeDtypeStruct((512, 512), BF16),
            jax.ShapeDtypeStruct((256, 384), BF16),
        ),
        in_specs=[SMEM, SMEM, HBM, HBM],
        out_specs=(VMEM,) * 9,
        scratch_shapes=[
            pltpu.VMEM((6, 64, 512), F32),
            pltpu.VMEM((36, 16, 128), F32),
            pltpu.SemaphoreType.DMA((2,)),
        ],
        compiler_params=PARAMS,
        cost_estimate=pl.CostEstimate(flops=4_000_000, bytes_accessed=2_000_000, transcendentals=0),
        name="prep",
    )(place, diffusivity, state, coarse_map)


def const(consts_ref, r):
    return consts_ref[pl.ds(r, 1), :]


def strips_above_below(consts_ref, pair_rows_ref, cross_rows_ref):
    odd = jnp.broadcast_to(const(consts_ref, 0), (4, 128)) > 0.5
    pick = lambda a, b: lambda f, t: jnp.where(
        odd, a[f, :, 128 * t : 128 * t + 128], b[f, :, 128 * t : 128 * t + 128]
    )
    return pick(pair_rows_ref, cross_rows_ref), pick(cross_rows_ref, pair_rows_ref)


def corners_kernel(consts_ref, pair_rows_ref, cross_rows_ref, pair_in, cross_in, pair_ref, cross_ref):
    del pair_in, cross_in
    odd = jnp.broadcast_to(const(consts_ref, 1), (4, 128)) > 0.5
    above, below = strips_above_below(consts_ref, pair_rows_ref, cross_rows_ref)
    for at, piece in ((64, below), (68, above)):
        right, left = messages(piece, 4)
        pair_ref[at : at + 4, :] = jnp.where(odd, left, right)
        cross_ref[at : at + 4, :] = jnp.where(odd, right, left)


def corners(consts, pair_rows, cross_rows, pair_columns, cross_columns):
    out = jax.ShapeDtypeStruct((72, 128), F32)
    return pl.pallas_call(
        corners_kernel,
        out_shape=(out, out),
        in_specs=[VMEM] * 5,
        out_specs=(VMEM, VMEM),
        input_output_aliases={3: 0, 4: 1},
        compiler_params=PARAMS,
        name="corners",
    )(consts, pair_rows, cross_rows, pair_columns, cross_columns)


def middle_kernel(nu_ref, consts_ref, weights_ref, order_ref, cells_ref, pair_rows_ref, cross_rows_ref, packed_in,
                  strips_in, fine_ref, packed_ref, strips_ref, buffer, face, halo, flat):
    del packed_in, strips_in
    above, below = strips_above_below(consts_ref, pair_rows_ref, cross_rows_ref)
    for f in range(6):
        for t in range(4):
            halo[8 * f : 8 * f + 4, 128 * t : 128 * t + 128] = above(f, t)
            halo[8 * f + 4 : 8 * f + 8, 128 * t : 128 * t + 128] = below(f, t)
    put_strips(strips_ref, 64, below, 4)
    put_strips(strips_ref, 68, above, 4)
    ordered = split_dot(halo[...], order_ref[...])
    for f in range(6):
        for k in range(4):
            buffer[0, f, k, TOP : TOP + 64, :] = cells_ref[f, k]
            piece = ordered[8 * f : 8 * f + 8, 128 * k : 128 * k + 128]
            buffer[0, f, k, TOP - 4 : TOP, :] = piece[0:4]
            buffer[0, f, k, TOP + 64 : TOP + 68, :] = piece[4:8]
    has_above = jnp.broadcast_to(const(consts_ref, 2), (8, 128)) > 0.5
    has_below = jnp.broadcast_to(const(consts_ref, 3), (8, 128)) > 0.5

    def step_cells(now, later, tiles, last):
        for i in tiles:
            rows = pl.ds(8 * i, 8)
            speed = [FACE * jnp.tanh(buffer[now, 1, k, rows, :]) for k in range(4)]
            face[0, rows, :] = speed[0] + pltpu.roll(speed[3], 1, 1)
            for k in range(4):
                face[k + 1, rows, :] = speed[k] + (speed[k + 1] if k < 3 else pltpu.roll(speed[0], 127, 1))
            for k in range(4):
                face[5 + k, rows, :] = face[k, rows, :] - face[k + 1, rows, :]
        for f in range(6):
            rate = STEP * nu_ref[f]
            keep = 1.0 - 4.0 * rate
            for i in tiles:
                rows = pl.ds(8 * i, 8)
                center = [buffer[now, f, k, rows, :] for k in range(4)]
                east = center[1:] + [pltpu.roll(center[0], 127, 1)]
                west = [pltpu.roll(center[3], 1, 1)] + center[:3]
                up, down = rate * weights_ref[0, rows, :], rate * weights_ref[1, rows, :]
                for k in range(4):
                    north = buffer[now, f, k, pl.ds(8 * i + 1, 8), :]
                    south = buffer[now, f, k, pl.ds(8 * i - 1, 8), :]
                    new = (up * north + down * south) + (
                        (east[k] * (rate - face[k + 1, rows, :]) + west[k] * (rate + face[k, rows, :]))
                        + center[k] * (keep + face[5 + k, rows, :])
                    )
                    if i == 1:
                        new = jnp.where(has_above, new, F32(0.0))
                    if i == 10:
                        new = jnp.where(has_below, new, F32(0.0))
                    buffer[later, f, k, rows, :] = new
                    if last:
                        at = 64 * f + 8 * i - TOP
                        flat[at : at + 8, 128 * k : 128 * k + 128] = new

    for step in range(FSTEPS):
        last = step == FSTEPS - 1
        step_cells(step % 2, (step + 1) % 2, range(2, 10) if last else range(1, 11), last)
    slot = FSTEPS % 2
    put_means(packed_ref, 18, lambda f, k, r: buffer[slot, f, k, pl.ds(TOP + r, 16, stride=4), :], True)
    fine_ref[...] = split_dot(flat[...], order_ref[...], transposed=True).reshape(6, 64, 512)


def middle(diffusivity, consts, weights, order, cells, pair_rows, cross_rows, packed, strips):
    return pl.pallas_call(
        middle_kernel,
        out_shape=(
            jax.ShapeDtypeStruct((6, 64, 512), F32),
            jax.ShapeDtypeStruct((768, 128), F32),
            jax.ShapeDtypeStruct((3, 72, 128), F32),
        ),
        in_specs=[SMEM] + [VMEM] * 8,
        out_specs=(VMEM,) * 3,
        scratch_shapes=[
            pltpu.VMEM((2, 6, 4, BUF, 128), F32),
            pltpu.VMEM((9, BUF, 128), F32),
            pltpu.VMEM((48, 512), F32),
            pltpu.VMEM((384, 512), F32),
        ],
        input_output_aliases={7: 1, 8: 2},
        compiler_params=PARAMS,
        cost_estimate=pl.CostEstimate(flops=20_000_000, bytes_accessed=4_000_000, transcendentals=200_000),
        name="middle",
    )(diffusivity, consts, weights, order, cells, pair_rows, cross_rows, packed, strips)


def sides_kernel(consts_ref, weights_ref, spread_ref, strips_ref, pair_ref, cross_ref, packed_in,
                 edge_ref, packed_ref, buffer, face):
    full = lambda r, count=8: jnp.broadcast_to(const(consts_ref, r), (count, 128))
    for source, target, count in ((0, TOP, 64), (64, TOP + 64, 4), (68, TOP - 4, 4)):
        at = lanes((count, 128)) % 32
        odd = full(1, count) > 0.5
        pair, cross = pair_ref[source : source + count, :], cross_ref[source : source + count, :]
        from_left, from_right = jnp.where(odd, pair, cross), jnp.where(odd, cross, pair)
        for tile in range(3):
            value = jnp.where(at < 4, moved(from_left, -4 * tile), strips_ref[tile, source : source + count, :])
            value = jnp.where((at >= 24) & (at < 28), moved(from_right, 4 * tile), value)
            buffer[0, tile, target : target + count, :] = value
    has_above, has_below, inside = full(2) > 0.5, full(3) > 0.5, full(4) > 0.5
    rates = [full(5 + tile) for tile in range(3)]
    keeps = [1.0 - 4.0 * rate for rate in rates]
    for step in range(FSTEPS):
        now, later = step % 2, (step + 1) % 2
        last = step == FSTEPS - 1
        tiles = range(2, 10) if last else range(1, 11)
        for i in tiles:
            rows = pl.ds(8 * i, 8)
            speed = FACE * jnp.tanh(buffer[now, 2, rows, :])
            face[0, rows, :] = speed + pltpu.roll(speed, 127, 1)
            face[1, rows, :] = speed + pltpu.roll(speed, 1, 1)
        for i in tiles:
            rows = pl.ds(8 * i, 8)
            up, down = weights_ref[0, rows, :], weights_ref[1, rows, :]
            fe, fw = face[0, rows, :], face[1, rows, :]
            for tile in range(2 if last else 3):
                rate = rates[tile]
                center = buffer[now, tile, rows, :]
                north = buffer[now, tile, pl.ds(8 * i + 1, 8), :]
                south = buffer[now, tile, pl.ds(8 * i - 1, 8), :]
                new = rate * (up * north + down * south) + (
                    (pltpu.roll(center, 127, 1) * (rate - fe) + pltpu.roll(center, 1, 1) * (rate + fw))
                    + center * (keeps[tile] + (fw - fe))
                )
                if i == 1:
                    new = jnp.where(has_above, new, F32(0.0))
                if i == 10:
                    new = jnp.where(has_below, new, F32(0.0))
                new = jnp.where(inside, new, F32(0.0))
                buffer[later, tile, rows, :] = new
                if last:
                    edge_ref[tile, 8 * i - TOP : 8 * i - TOP + 8, :] = new
    slot = FSTEPS % 2
    sums = []
    for tile in range(2):
        load = lambda r: buffer[slot, tile, pl.ds(TOP + r, 16, stride=4), :]
        sums.append((load(0) + load(1)) + (load(2) + load(3)))
    own = split_dot(jnp.concatenate(sums, axis=1), spread_ref[...])
    left = lanes((16, 128)) % 64 == 0
    for j in range(3):
        piece = own[:, 128 * j : 128 * j + 128]
        even, odd = pl.ds(18 + j, 16, stride=48), pl.ds(42 + j, 16, stride=48)
        packed_ref[even, :] = packed_in[even, :] + jnp.where(left, piece, F32(0.0))
        packed_ref[odd, :] = packed_in[odd, :] + jnp.where(left, F32(0.0), piece)


def sides(consts, weights, spread, strips, pair_columns, cross_columns, packed):
    return pl.pallas_call(
        sides_kernel,
        out_shape=(jax.ShapeDtypeStruct((2, 64, 128), F32), jax.ShapeDtypeStruct((768, 128), F32)),
        in_specs=[VMEM] * 7,
        out_specs=(VMEM, VMEM),
        scratch_shapes=[pltpu.VMEM((2, 3, BUF, 128), F32), pltpu.VMEM((2, BUF, 128), F32)],
        input_output_aliases={6: 1},
        compiler_params=PARAMS,
        name="sides",
    )(consts, weights, spread, strips, pair_columns, cross_columns, packed)


def scan_kernel(slices, packed_ref, mapped_ref, other, rows):
    other[...] = pltpu.roll(packed_ref[...], 64, 1)
    carry = [jnp.zeros((1, 128), F32)] * 6
    for n in range(slices):
        base = 24 * n
        line = lambda k, half: (other if half else packed_ref)[pl.ds(base + k, 1), :]
        mapped = []
        for f in range(6):
            terms = [line(3 * f + g % 3, g >= 3) * carry[g] for g in range(6)]
            total = (terms[0] + terms[1]) + (terms[2] + terms[3]) + (terms[4] + terms[5])
            rows[f, pl.ds(n, 1), :] = total
            mapped.append(total)
        if n < slices - 1:
            carry = [mapped[f] + (line(18 + f % 3, f >= 3) - line(45 + f % 3, f >= 3)) for f in range(6)]
    left = lanes((slices, 128)) < 64
    for j in range(3):
        mapped_ref[pl.ds(j, slices, stride=4), :] = jnp.where(left, rows[j], pltpu.roll(rows[j + 3], 64, 1))


def scanned(packed, slices):
    return pl.pallas_call(
        functools.partial(scan_kernel, slices),
        out_shape=jax.ShapeDtypeStruct((4 * slices, 128), F32),
        in_specs=[VMEM],
        out_specs=VMEM,
        scratch_shapes=[pltpu.VMEM((24 * slices, 128), F32), pltpu.VMEM((6, slices, 128), F32)],
        compiler_params=PARAMS,
        name="scan",
    )(packed)


def final_kernel(fine_ref, edge_ref, mapped_ref, out_ref, wide, done, sems):
    left = lanes((16, 128)) < 64
    upper = lax.broadcasted_iota(jnp.int32, (8, 128), 0) < 4
    lane = lanes((8, 128))
    for f in range(6):
        j = f % 3
        even = mapped_ref[pl.ds(j, 16, stride=8), :]
        odd = mapped_ref[pl.ds(4 + j, 16, stride=8), :]
        if f < 3:
            cells = jnp.where(left, even, pltpu.roll(odd, 64, 1))
        else:
            cells = jnp.where(left, pltpu.roll(even, 64, 1), odd)
        for t in range(4):
            source = 32 * t + lanes((16, 128)) // 4
            wide[f, t] = jnp.take_along_axis(cells, source, axis=1)
    copies = []
    for f in range(6):
        tile, base = f // 4, 32 * (f % 4)
        for t in range(4):
            cut = slice(128 * t, 128 * t + 128)
            for q in range(8):
                first = jnp.broadcast_to(wide[f, t, pl.ds(2 * q, 1), :], (8, 128))
                second = jnp.broadcast_to(wide[f, t, pl.ds(2 * q + 1, 1), :], (8, 128))
                rows = slice(8 * q, 8 * q + 8)
                own = fine_ref[f, rows, cut]
                if t == 0:
                    own = jnp.where(lane < 4, moved(edge_ref[tile, rows, :], -(base + 4)), own)
                if t == 3:
                    own = jnp.where(lane >= 124, moved(edge_ref[tile, rows, :], 104 - base), own)
                done[f, rows, cut] = own + jnp.where(upper, first, second)
        copies.append(pltpu.make_async_copy(done.at[f], out_ref.at[f], sems.at[f]))
        copies[f].start()
    for copy in copies:
        copy.wait()


def final(fine_state, edge, mapped):
    return pl.pallas_call(
        final_kernel,
        out_shape=jax.ShapeDtypeStruct((6, 64, 512), F32),
        in_specs=[VMEM] * 3,
        out_specs=HBM,
        scratch_shapes=[
            pltpu.VMEM((6, 4, 16, 128), F32),
            pltpu.VMEM((6, 64, 512), F32),
            pltpu.SemaphoreType.DMA((6,)),
        ],
        compiler_params=PARAMS,
        name="final",
    )(fine_state, edge, mapped)


def swapped(pair, cross, axis):
    size = lax.axis_size(axis)
    couples = lambda first: [(i, i + 1) for i in range(first, size - 1, 2)]
    both = lambda links: links + [(b, a) for a, b in links]
    return lax.ppermute(pair, axis, both(couples(0))), lax.ppermute(cross, axis, both(couples(1)))


def local(starts, coarse_map, diffusivity):
    state = pltpu.with_memory_space_constraint(starts[0], pltpu.HBM)
    entries = pltpu.with_memory_space_constraint(coarse_map[0], pltpu.HBM)
    slices = lax.axis_size("tm")
    row = lax.axis_index("row")
    place = jnp.stack([row, lax.axis_index("gz")]).astype(jnp.int32)
    first, last = starts[0, :, :4, :], starts[0, :, 60:, :]
    odd = row % 2 == 1
    pair_rows, cross_rows = swapped(jnp.where(odd, first, last), jnp.where(odd, last, first), "row")
    cells, packed, pair_columns, cross_columns, strips, consts, weights, order, spread = prep(
        place, diffusivity, state, entries
    )
    pair_columns, cross_columns = corners(consts, pair_rows, cross_rows, pair_columns, cross_columns)
    pair_columns, cross_columns = swapped(pair_columns, cross_columns, "gz")
    fine_state, packed, strips = middle(
        diffusivity, consts, weights, order, cells, pair_rows, cross_rows, packed, strips
    )
    edge, packed = sides(consts, weights, spread, strips, pair_columns, cross_columns, packed)
    packed = lax.all_to_all(packed, "tm", 0, 0, tiled=True)
    mapped = scanned(packed, slices)
    mapped = lax.all_to_all(mapped, "tm", 0, 0, tiled=True)
    return final(fine_state, edge, mapped)[None]


def solution(mesh):
    placed = (P("tm", None, "row", "gz"), P("tm", None, "row", "gz"), P())
    return jax.shard_map(
        local, mesh=mesh, in_specs=placed, out_specs=P("tm", None, "row", "gz"), check_vma=False
    )
```

time: 516 us -> 70.1 us (0.14)
  the two profiles are of different devices: /device:TPU:96 before, /device:TPU:1 now
where the time goes in v2:
time: 70.1 us; the launch traced here: 69.8 us
  blocking collectives  45.5 us (65%)
  starting transfers between devices  14.1 us (20%)
  Pallas kernels  8.37 us (12%)
  other arithmetic  1.04 us (1%)
    all_to_all x1, blocking collectives, local(): packed = lax.all_to_all(packed, 'tm', 0, 0, tiled=True)  29.5 us
    all_to_all x1, blocking collectives, local(): mapped = lax.all_to_all(mapped, 'tm', 0, 0, tiled=True)  16 us
    ppermute x2, starting transfers between devices, swapped(): lax.ppermute(pair, axis, both(couples(0)))  11.4 us
    pallas_call x1, Pallas kernels, middle(): pl.pallas_call(middle_kernel, out_shape=(jax.ShapeDtypeStruct((6, 64, 512...  3.27 us
    ppermute x2, starting transfers between devices, swapped(): lax.ppermute(cross, axis, both(couples(1)))  2.72 us
    pallas_call x1, Pallas kernels, prep(): pl.pallas_call(prep_kernel, out_shape=(shape(6, 4, 64, 128), shape(768, 1...  2.58 us
  transfers between devices with their start and end apart: 4, of which 0 were waited for; matrix products, arithmetic and copies ran while one was open for 0% of the time, Pallas kernels for 8%

profile of v2, /device:TPU:1, one launch (start us, length us, event | category | flops | bytes accessed | tf_op | source)
XLA Modules:
  0.0 69.8 jit_solution(5558061608633364682)
XLA Ops:
  0.0 1.0 %select_bitcast_fusion = (f32[6,4,512]{2,1,0:T(4,128)S(1)}, f32[6,4,512]{2,1,0:T(4,128)S(1)}) fusion(f32[1,6,64,512]{3,2,1,0:T(8,128)} %param.3, pred[]{:T(512)S(6)} %eq.5), kind=kLoop, calls=%fused_computation | loop fusion | flops 24576 | bytes 196609 | tf_op jit(solution)/shard_map/jit(_where)/select_n | solution.py:456
  1.0 0.7 collective-permute-start.1
  1.6 6.4 %collective-permute-start = (f32[6,4,512]{2,1,0:T(4,128)S(1)}, f32[6,4,512]{2,1,0:T(4,128)S(1)}, u32[]{:S(2)}, u32[]{:S(2)}) collective-permute-start(f32[6,4,512]{2,1,0:T(4,128)S(1)} %get-tuple-element.38), channel_id=1, source_target_pairs={{0,1},{2,3},{1,0},{3,2},{4,5},{6,7},{5,4},{7,6},{8,9},{10,11},{9,8... | collective-permute-start | bytes 147464 | tf_op jit(solution)/shard_map/ppermute | solution.py:445
  8.0 0.1 pad_add_fusion.place_ref
  8.1 0.0 copy-start
  8.1 0.7 copy-done
  8.8 2.6 %prep.1 = (f32[6,4,64,128]{3,2,1,0:T(8,128)S(1)}, f32[768,128]{1,0:T(8,128)S(1)}, f32[72,128]{1,0:T(8,128)S(1)}, f32[72,128]{1,0:T(8,128)S(1)}, f32[3,72,128]{2,...) custom-call(s32[2]{0:T(128)S(1)} %pad_add_fusion.place_ref, ...), custom_call_target="tpu_custom_call" | custom-call | flops 4000000 | bytes 2000000 | tf_op jit(solution)/shard_map/prep/pallas_call | solution.py:140
  11.4 0.0 collective-permute-done.1.cross_rows_ref
  11.4 0.0 collective-permute-done.pair_rows_ref
  11.4 0.1 corners.1
  11.5 5.0 %collective-permute-start.2 = (f32[72,128]{1,0:T(8,128)S(1)}, f32[72,128]{1,0:T(8,128)S(1)}, u32[]{:S(2)}, u32[]{:S(2)}) collective-permute-start(f32[72,128]{1,0:T(8,128)S(1)} %get-tuple-element.32), channel_id=1, source_target_pairs={{0,4},{8,12},{4,0},{12,8},{1,5},{9,13},{5,1},{13,9},{2,6},{10,14},... | collective-permute-start | bytes 110600 | tf_op jit(solution)/shard_map/ppermute | solution.py:445
  16.5 2.1 %collective-permute-start.3 = (f32[72,128]{1,0:T(8,128)S(1)}, f32[72,128]{1,0:T(8,128)S(1)}, u32[]{:S(2)}, u32[]{:S(2)}) collective-permute-start(f32[72,128]{1,0:T(8,128)S(1)} %get-tuple-element.33), channel_id=1, source_target_pairs={{4,8},{8,4},{5,9},{9,5},{6,10},{10,6},{7,11},{11,7},{20,24},{24,20... | collective-permute-start | bytes 110600 | tf_op jit(solution)/shard_map/ppermute | solution.py:445
  18.5 3.3 %middle.1 = (f32[6,64,512]{2,1,0:T(8,128)S(1)}, f32[768,128]{1,0:T(8,128)S(1)}, f32[3,72,128]{2,1,0:T(8,128)S(1)}) custom-call(f32[6]{0:T(128)S(1)} %copy-done, f32[8,128]{1,0:T(8,128)S(1)} %get-tuple-element.21.consts_ref, f32[2,96,128]{2,1,0:T(8,128)S(1)} %get-tuple-element.22.weights_ref, ...), custom_call_target="tpu_custom_call", output_to_operand_aliasing={{1}: (7, {}), {2}: (8, {})} | custom-call | flops 20000000 | bytes 4000000 | tf_op jit(solution)/shard_map/middle/pallas_call | solution.py:264
  21.8 0.0 collective-permute-done.2.pair_ref
  21.8 0.0 collective-permute-done.3.cross_ref
  21.8 0.7 %sides.1 = (f32[2,64,128]{2,1,0:T(8,128)S(1)}, f32[768,128]{1,0:T(8,128)S(1)}) custom-call(f32[8,128]{1,0:T(8,128)S(1)} %get-tuple-element.21.consts_ref, f32[2,96,128]{2,1,0:T(8,128)S(1)} %get-tuple-element.22.weights_ref, bf16[256,384]{1,0:T(8,128)(2,1)S(1)} %get-tuple-element.28.spread_ref, ...), custom_call_target="tpu_custom_call", output_to_operand_aliasing={{1}: (6, {})} | custom-call | tf_op jit(solution)/shard_map/sides/pallas_call | solution.py:346
  22.6 29.5 %all_to_all.22 = f32[32,24,128]{2,1,0:T(8,128)S(1)} all-to-all(f32[32,24,128]{2,1,0:T(8,128)S(1)} %bitcast.13), channel_id=1, replica_groups=mesh['tm'=32,'gz'=4,'row'=4] {'tm'}, dimensions={0} | all-to-all | bytes 786432 | tf_op jit(solution)/shard_map/all_to_all | solution.py:466
  52.1 0.5 scan.1
  52.6 16.0 %all_to_all.23 = f32[32,4,128]{2,1,0:T(4,128)S(1)} all-to-all(f32[32,4,128]{2,1,0:T(4,128)S(1)} %bitcast.15), channel_id=1, replica_groups=mesh['tm'=32,'gz'=4,'row'=4] {'tm'}, dimensions={0} | all-to-all | bytes 131072 | tf_op jit(solution)/shard_map/all_to_all | solution.py:468
  68.6 1.2 %final.1 = f32[6,64,512]{2,1,0:T(8,128)} custom-call(f32[6,64,512]{2,1,0:T(8,128)S(1)} %get-tuple-element.27.fine_ref, f32[2,64,128]{2,1,0:T(8,128)S(1)} %get-tuple-element.35.edge_ref, f32[128,128]{1,0:T(8,128)S(1)} %bitcast.16), custom_call_target="tpu_custom_call" | custom-call | tf_op jit(solution)/shard_map/final/pallas_call | solution.py:426
Async XLA Ops:
  1.0 10.4 %collective-permute-start.1 = (f32[6,4,512]{2,1,0:T(4,128)S(1)}, f32[6,4,512]{2,1,0:T(4,128)S(1)}, u32[]{:S(2)}, u32[]{:S(2)}) collective-permute-start(f32[6,4,512]{2,1,0:T(4,128)S(1)} %get-tuple-element.37), channel_id=1, source_target_pairs={{1,2},{2,1},{5,6},{6,5},{9,10},{10,9},{13,14},{14,13},{17,18},{18,... | collective-permute-start | bytes 147464 | tf_op jit(solution)/shard_map/ppermute | solution.py:445
  1.6 9.7 %collective-permute-start = (f32[6,4,512]{2,1,0:T(4,128)S(1)}, f32[6,4,512]{2,1,0:T(4,128)S(1)}, u32[]{:S(2)}, u32[]{:S(2)}) collective-permute-start(f32[6,4,512]{2,1,0:T(4,128)S(1)} %get-tuple-element.38), channel_id=1, source_target_pairs={{0,1},{2,3},{1,0},{3,2},{4,5},{6,7},{5,4},{7,6},{8,9},{10,11},{9,8... | collective-permute-start | bytes 147464 | tf_op jit(solution)/shard_map/ppermute | solution.py:445
  8.1 0.7 copy-start
  11.5 10.3 %collective-permute-start.2 = (f32[72,128]{1,0:T(8,128)S(1)}, f32[72,128]{1,0:T(8,128)S(1)}, u32[]{:S(2)}, u32[]{:S(2)}) collective-permute-start(f32[72,128]{1,0:T(8,128)S(1)} %get-tuple-element.32), channel_id=1, source_target_pairs={{0,4},{8,12},{4,0},{12,8},{1,5},{9,13},{5,1},{13,9},{2,6},{10,14},... | collective-permute-start | bytes 110600 | tf_op jit(solution)/shard_map/ppermute | solution.py:445
  16.5 5.4 %collective-permute-start.3 = (f32[72,128]{1,0:T(8,128)S(1)}, f32[72,128]{1,0:T(8,128)S(1)}, u32[]{:S(2)}, u32[]{:S(2)}) collective-permute-start(f32[72,128]{1,0:T(8,128)S(1)} %get-tuple-element.33), channel_id=1, source_target_pairs={{4,8},{8,4},{5,9},{9,5},{6,10},{10,6},{7,11},{11,7},{20,24},{24,20... | collective-permute-start | bytes 110600 | tf_op jit(solution)/shard_map/ppermute | solution.py:445

commit v3 on v2

--- a/solution.py
+++ b/solution.py
@@ -68,13 +68,13 @@
         strips_ref[tile, rows : rows + count, :] = total
 
 
-def prep_kernel(place_ref, nu_ref, starts_ref, map_ref, cells_ref, packed_ref, pair_ref, cross_ref, strips_ref,
-                consts_ref, weights_ref, order_ref, spread_ref, state, entries, sems):
-    row, column = place_ref[0], place_ref[1]
-    state_copy = pltpu.make_async_copy(starts_ref, state, sems.at[0])
-    map_copy = pltpu.make_async_copy(map_ref, entries, sems.at[1])
-    state_copy.start()
-    map_copy.start()
+def load_kernel(nu_hbm, starts_ref, state_ref, pair_ref, cross_ref, consts_ref, weights_ref, order_ref, spread_ref, nu_ref, sems):
+    outer = [pl.ds(0, 8), pl.ds(56, 8), pl.ds(8, 48)]
+    copies = [pltpu.make_async_copy(starts_ref.at[:, r, :], state_ref.at[:, r, :], sems.at[i]) for i, r in enumerate(outer)]
+    copies.append(pltpu.make_async_copy(nu_hbm, nu_ref, sems.at[3]))
+    for copy in copies:
+        copy.start()
+    row, column = lax.axis_index("row"), lax.axis_index("gz")
     for t in range(4):
         z = lax.broadcasted_iota(jnp.int32, (128, 512), 0) + 128 * t
         place = lax.broadcasted_iota(jnp.int32, (128, 512), 1)
@@ -86,31 +86,65 @@
     to = jnp.where((at >= 4) & (at < 8), base, jnp.where((at >= 20) & (at < 24), base + 63, -1))
     to = jnp.where(field < 6, to, -1)
     spread_ref[...] = jnp.where(to == target, F32(1.0 / 16.0), F32(0.0)).astype(BF16)
-    line, lane = lax.broadcasted_iota(jnp.int32, (8, 128), 0), lanes((8, 128))
+    radius = (lax.broadcasted_iota(jnp.int32, (BUF, 128), 0) - TOP + row * 64).astype(F32)
+    weights_ref[0] = (radius + 1.0) / (radius + 0.5)
+    weights_ref[1] = radius / (radius + 0.5)
+    copies[3].wait()
+    line, lane = lax.broadcasted_iota(jnp.int32, (16, 128), 0), lanes((16, 128))
     flag = lambda condition: jnp.where(condition, F32(1.0), F32(0.0))
     group, at = lane // 32, lane % 32
     low, high = jnp.where(column > 0, 0, 4), jnp.where(column < 3, 32, 24)
     rates = lambda fields: functools.reduce(
-        lambda a, q: jnp.where(group == q, STEP * nu_ref[fields[q]], a), range(4), jnp.zeros((8, 128), F32)
+        lambda a, q: jnp.where(group == q, STEP * nu_ref[fields[q]], a), range(4), jnp.zeros((16, 128), F32)
     )
     values = [flag(row % 2 == 1), flag(column % 2 == 1), flag(row > 0), flag(row < 3)]
     values += [flag((at >= low) & (at < high)), rates((0, 1, 2, 3)), rates((4, 5, 5, 5)), rates((1, 1, 1, 1))]
-    total = jnp.zeros((8, 128), F32)
+    values += [rates((f, f, f, f)) for f in range(6)]
+    total = jnp.zeros((16, 128), F32)
     for r, value in enumerate(values):
         total = jnp.where(line == r, value, total)
     consts_ref[...] = total
-    radius = (lax.broadcasted_iota(jnp.int32, (BUF, 128), 0) - TOP + row * 64).astype(F32)
-    weights_ref[0] = (radius + 1.0) / (radius + 0.5)
-    weights_ref[1] = radius / (radius + 0.5)
-
-    state_copy.wait()
-    piece = lambda f, t: state[f, :, 128 * t : 128 * t + 128]
-    odd = column % 2 == 1
+    copies[0].wait()
+    copies[1].wait()
+    odd = row % 2 == 1
+    for f in range(6):
+        first, last = state_ref[f, 0:4, :], state_ref[f, 60:64, :]
+        pair_ref[f] = jnp.where(odd, first, last)
+        cross_ref[f] = jnp.where(odd, last, first)
+    copies[2].wait()
+
+
+def load(diffusivity, state):
+    shape = lambda *dims: jax.ShapeDtypeStruct(dims, F32)
+    return pl.pallas_call(
+        load_kernel,
+        out_shape=(
+            shape(6, 64, 512),
+            shape(6, 4, 512),
+            shape(6, 4, 512),
+            shape(16, 128),
+            shape(2, BUF, 128),
+            jax.ShapeDtypeStruct((512, 512), BF16),
+            jax.ShapeDtypeStruct((256, 384), BF16),
+        ),
+        in_specs=[HBM, HBM],
+        out_specs=(VMEM,) * 7,
+        scratch_shapes=[pltpu.SMEM((6,), F32), pltpu.SemaphoreType.DMA((4,))],
+        compiler_params=PARAMS,
+        name="load",
+    )(diffusivity, state)
+
+
+def prep_kernel(consts_ref, order_ref, state_ref, map_ref, cells_ref, packed_ref, pair_ref, cross_ref, strips_ref, entries, sem):
+    map_copy = pltpu.make_async_copy(map_ref, entries, sem)
+    map_copy.start()
+    piece = lambda f, t: state_ref[f, :, 128 * t : 128 * t + 128]
+    odd = jnp.broadcast_to(const(consts_ref, 1), (64, 128)) > 0.5
     right, left = messages(piece, 64)
     pair_ref[0:64, :] = jnp.where(odd, left, right)
     cross_ref[0:64, :] = jnp.where(odd, right, left)
     put_strips(strips_ref, 0, piece, 64)
-    ordered = split_dot(state[...].reshape(384, 512), order_ref[...])
+    ordered = split_dot(state_ref[...].reshape(384, 512), order_ref[...])
     for f in range(6):
         for k in range(4):
             cells_ref[f, k] = ordered[64 * f : 64 * f + 64, 128 * k : 128 * k + 128]
@@ -135,32 +169,18 @@
         put_pair(packed_ref, at + j, means[j], means[j + 3])
 
 
-def prep(place, diffusivity, state, coarse_map):
+def prep(consts, order, state, coarse_map):
     shape = lambda *dims: jax.ShapeDtypeStruct(dims, F32)
     return pl.pallas_call(
         prep_kernel,
-        out_shape=(
-            shape(6, 4, 64, 128),
-            shape(768, 128),
-            shape(72, 128),
-            shape(72, 128),
-            shape(3, 72, 128),
-            shape(8, 128),
-            shape(2, BUF, 128),
-            jax.ShapeDtypeStruct((512, 512), BF16),
-            jax.ShapeDtypeStruct((256, 384), BF16),
-        ),
-        in_specs=[SMEM, SMEM, HBM, HBM],
-        out_specs=(VMEM,) * 9,
-        scratch_shapes=[
-            pltpu.VMEM((6, 64, 512), F32),
-            pltpu.VMEM((36, 16, 128), F32),
-            pltpu.SemaphoreType.DMA((2,)),
-        ],
+        out_shape=(shape(6, 4, 64, 128), shape(768, 128), shape(72, 128), shape(72, 128), shape(3, 72, 128)),
+        in_specs=[VMEM, VMEM, VMEM, HBM],
+        out_specs=(VMEM,) * 5,
+        scratch_shapes=[pltpu.VMEM((36, 16, 128), F32), pltpu.SemaphoreType.DMA(())],
         compiler_params=PARAMS,
         cost_estimate=pl.CostEstimate(flops=4_000_000, bytes_accessed=2_000_000, transcendentals=0),
         name="prep",
-    )(place, diffusivity, state, coarse_map)
+    )(consts, order, state, coarse_map)
 
 
 def const(consts_ref, r):
@@ -198,7 +218,7 @@
     )(consts, pair_rows, cross_rows, pair_columns, cross_columns)
 
 
-def middle_kernel(nu_ref, consts_ref, weights_ref, order_ref, cells_ref, pair_rows_ref, cross_rows_ref, packed_in,
+def middle_kernel(consts_ref, weights_ref, order_ref, cells_ref, pair_rows_ref, cross_rows_ref, packed_in,
                   strips_in, fine_ref, packed_ref, strips_ref, buffer, face, halo, flat):
     del packed_in, strips_in
     above, below = strips_above_below(consts_ref, pair_rows_ref, cross_rows_ref)
@@ -228,7 +248,7 @@
             for k in range(4):
                 face[5 + k, rows, :] = face[k, rows, :] - face[k + 1, rows, :]
         for f in range(6):
-            rate = STEP * nu_ref[f]
+            rate = jnp.broadcast_to(const(consts_ref, 8 + f), (8, 128))
             keep = 1.0 - 4.0 * rate
             for i in tiles:
                 rows = pl.ds(8 * i, 8)
@@ -260,7 +280,7 @@
     fine_ref[...] = split_dot(flat[...], order_ref[...], transposed=True).reshape(6, 64, 512)
 
 
-def middle(diffusivity, consts, weights, order, cells, pair_rows, cross_rows, packed, strips):
+def middle(consts, weights, order, cells, pair_rows, cross_rows, packed, strips):
     return pl.pallas_call(
         middle_kernel,
         out_shape=(
@@ -268,7 +288,7 @@
             jax.ShapeDtypeStruct((768, 128), F32),
             jax.ShapeDtypeStruct((3, 72, 128), F32),
         ),
-        in_specs=[SMEM] + [VMEM] * 8,
+        in_specs=[VMEM] * 8,
         out_specs=(VMEM,) * 3,
         scratch_shapes=[
             pltpu.VMEM((2, 6, 4, BUF, 128), F32),
@@ -276,11 +296,11 @@
             pltpu.VMEM((48, 512), F32),
             pltpu.VMEM((384, 512), F32),
         ],
-        input_output_aliases={7: 1, 8: 2},
+        input_output_aliases={6: 1, 7: 2},
         compiler_params=PARAMS,
         cost_estimate=pl.CostEstimate(flops=20_000_000, bytes_accessed=4_000_000, transcendentals=200_000),
         name="middle",
-    )(diffusivity, consts, weights, order, cells, pair_rows, cross_rows, packed, strips)
+    )(consts, weights, order, cells, pair_rows, cross_rows, packed, strips)
 
 
 def sides_kernel(consts_ref, weights_ref, spread_ref, strips_ref, pair_ref, cross_ref, packed_in,
@@ -446,22 +466,14 @@
 
 
 def local(starts, coarse_map, diffusivity):
-    state = pltpu.with_memory_space_constraint(starts[0], pltpu.HBM)
-    entries = pltpu.with_memory_space_constraint(coarse_map[0], pltpu.HBM)
+    in_hbm = lambda x: pltpu.with_memory_space_constraint(x, pltpu.HBM)
     slices = lax.axis_size("tm")
-    row = lax.axis_index("row")
-    place = jnp.stack([row, lax.axis_index("gz")]).astype(jnp.int32)
-    first, last = starts[0, :, :4, :], starts[0, :, 60:, :]
-    odd = row % 2 == 1
-    pair_rows, cross_rows = swapped(jnp.where(odd, first, last), jnp.where(odd, last, first), "row")
-    cells, packed, pair_columns, cross_columns, strips, consts, weights, order, spread = prep(
-        place, diffusivity, state, entries
-    )
+    state, pair_rows, cross_rows, consts, weights, order, spread = load(in_hbm(diffusivity), in_hbm(starts[0]))
+    pair_rows, cross_rows = swapped(pair_rows, cross_rows, "row")
+    cells, packed, pair_columns, cross_columns, strips = prep(consts, order, state, in_hbm(coarse_map[0]))
     pair_columns, cross_columns = corners(consts, pair_rows, cross_rows, pair_columns, cross_columns)
     pair_columns, cross_columns = swapped(pair_columns, cross_columns, "gz")
-    fine_state, packed, strips = middle(
-        diffusivity, consts, weights, order, cells, pair_rows, cross_rows, packed, strips
-    )
+    fine_state, packed, strips = middle(consts, weights, order, cells, pair_rows, cross_rows, packed, strips)
     edge, packed = sides(consts, weights, spread, strips, pair_columns, cross_columns, packed)
     packed = lax.all_to_all(packed, "tm", 0, 0, tiled=True)
     mapped = scanned(packed, slices)

time: 70.1 us -> 68.8 us (0.981)
  the two profiles are of different devices: /device:TPU:1 before, /device:TPU:4 now
where the time goes in v3:
time: 68.8 us; the launch traced here: 68.5 us
  blocking collectives  47 us (68%)
  starting transfers between devices  12.8 us (19%)
  Pallas kernels  8.09 us (12%)
    all_to_all x1, blocking collectives, local(): packed = lax.all_to_all(packed, 'tm', 0, 0, tiled=True)  28.2 us
    all_to_all x1, blocking collectives, local(): mapped = lax.all_to_all(mapped, 'tm', 0, 0, tiled=True)  18.8 us
    ppermute x2, starting transfers between devices, swapped(): lax.ppermute(cross, axis, both(couples(1)))  7.79 us
    ppermute x2, starting transfers between devices, swapped(): lax.ppermute(pair, axis, both(couples(0)))  5.03 us
    pallas_call x1, Pallas kernels, middle(): pl.pallas_call(middle_kernel, out_shape=(jax.ShapeDtypeStruct((6, 64, 512...  2.78 us
    pallas_call x1, Pallas kernels, prep(): pl.pallas_call(prep_kernel, out_shape=(shape(6, 4, 64, 128), shape(768, 1...  1.58 us
  transfers between devices with their start and end apart: 4, of which 1 were waited for; matrix products, arithmetic and copies ran while one was open for 0% of the time, Pallas kernels for 6%

profile of v3, /device:TPU:4, one launch (start us, length us, event | category | flops | bytes accessed | tf_op | source)
XLA Modules:
  0.0 68.5 jit_solution(15559524323079706069)
XLA Ops:
  0.0 1.2 %load.1 = (f32[6,64,512]{2,1,0:T(8,128)S(1)}, f32[6,4,512]{2,1,0:T(4,128)S(1)}, f32[6,4,512]{2,1,0:T(4,128)S(1)}, f32[16,128]{1,0:T(8,128)S(1)}, f32[2,96,128]{2...) custom-call(f32[6]{0:T(128)} %nu_hbm.1, f32[6,64,512]{2,1,0:T(8,128)} %bitcast.11), custom_call_target="tpu_custom_call" | custom-call | tf_op jit(solution)/shard_map/load/pallas_call | solution.py:119
  1.2 3.1 %collective-permute-start = (f32[6,4,512]{2,1,0:T(4,128)S(1)}, f32[6,4,512]{2,1,0:T(4,128)S(1)}, u32[]{:S(2)}, u32[]{:S(2)}) collective-permute-start(f32[6,4,512]{2,1,0:T(4,128)S(1)} %get-tuple-element.29), channel_id=1, source_target_pairs={{0,1},{2,3},{1,0},{3,2},{4,5},{6,7},{5,4},{7,6},{8,9},{10,11},{9,8... | collective-permute-start | bytes 147464 | tf_op jit(solution)/shard_map/ppermute | solution.py:465
  4.3 7.1 %collective-permute-start.1 = (f32[6,4,512]{2,1,0:T(4,128)S(1)}, f32[6,4,512]{2,1,0:T(4,128)S(1)}, u32[]{:S(2)}, u32[]{:S(2)}) collective-permute-start(f32[6,4,512]{2,1,0:T(4,128)S(1)} %get-tuple-element.30), channel_id=1, source_target_pairs={{1,2},{2,1},{5,6},{6,5},{9,10},{10,9},{13,14},{14,13},{17,18},{18,... | collective-permute-start | bytes 147464 | tf_op jit(solution)/shard_map/ppermute | solution.py:465
  11.5 1.6 %prep.1 = (f32[6,4,64,128]{3,2,1,0:T(8,128)S(1)}, f32[768,128]{1,0:T(8,128)S(1)}, f32[72,128]{1,0:T(8,128)S(1)}, f32[72,128]{1,0:T(8,128)S(1)}, f32[3,72,128]{2,1,0:T(8,128)S(1)}) custom-call(f32[16,128]{1,0:T(8,128)S(1)} %get-tuple-element.24.consts_ref, bf16[512,512]{1,0:T(8,128)(2,1)S(1)} %get-tuple-element.26.order_ref, ...), custom_call_target="tpu_custom_call" | custom-call | flops 4000000 | bytes 2000000 | tf_op jit(solution)/shard_map/prep/pallas_call | solution.py:174
  13.1 0.0 collective-permute-done.pair_rows_ref
  13.1 0.5 collective-permute-done.1.cross_rows_ref
  13.5 0.1 corners.1
  13.6 1.9 %collective-permute-start.2 = (f32[72,128]{1,0:T(8,128)S(1)}, f32[72,128]{1,0:T(8,128)S(1)}, u32[]{:S(2)}, u32[]{:S(2)}) collective-permute-start(f32[72,128]{1,0:T(8,128)S(1)} %get-tuple-element.38), channel_id=1, source_target_pairs={{0,4},{8,12},{4,0},{12,8},{1,5},{9,13},{5,1},{13,9},{2,6},{10,14},... | collective-permute-start | bytes 110600 | tf_op jit(solution)/shard_map/ppermute | solution.py:465
  15.6 0.7 collective-permute-start.3
  16.2 2.8 %middle.1 = (f32[6,64,512]{2,1,0:T(8,128)S(1)}, f32[768,128]{1,0:T(8,128)S(1)}, f32[3,72,128]{2,1,0:T(8,128)S(1)}) custom-call(f32[16,128]{1,0:T(8,128)S(1)} %get-tuple-element.24.consts_ref, f32[2,96,128]{2,1,0:T(8,128)S(1)} %get-tuple-element.25.weights_ref, ...), custom_call_target="tpu_custom_call", output_to_operand_aliasing={{1}: (6, {}), {2}: (7, {})} | custom-call | flops 20000000 | bytes 4000000 | tf_op jit(solution)/shard_map/middle/pallas_call | solution.py:284
  19.0 0.0 collective-permute-done.2.pair_ref
  19.0 0.0 collective-permute-done.3.cross_ref
  19.0 0.7 %sides.1 = (f32[2,64,128]{2,1,0:T(8,128)S(1)}, f32[768,128]{1,0:T(8,128)S(1)}) custom-call(f32[16,128]{1,0:T(8,128)S(1)} %get-tuple-element.24.consts_ref, f32[2,96,128]{2,1,0:T(8,128)S(1)} %get-tuple-element.25.weights_ref, bf16[256,384]{1,0:T(8,128)(2,1)S(1)} %get-tuple-element.34.spread_ref, ...), custom_call_target="tpu_custom_call", output_to_operand_aliasing={{1}: (6, {})} | custom-call | tf_op jit(solution)/shard_map/sides/pallas_call | solution.py:366
  19.8 28.2 %all_to_all.22 = f32[32,24,128]{2,1,0:T(8,128)S(1)} all-to-all(f32[32,24,128]{2,1,0:T(8,128)S(1)} %bitcast.7), channel_id=1, replica_groups=mesh['tm'=32,'gz'=4,'row'=4] {'tm'}, dimensions={0} | all-to-all | bytes 786432 | tf_op jit(solution)/shard_map/all_to_all | solution.py:478
  48.0 0.5 scan.1
  48.5 18.8 %all_to_all.23 = f32[32,4,128]{2,1,0:T(4,128)S(1)} all-to-all(f32[32,4,128]{2,1,0:T(4,128)S(1)} %bitcast.9), channel_id=1, replica_groups=mesh['tm'=32,'gz'=4,'row'=4] {'tm'}, dimensions={0} | all-to-all | bytes 131072 | tf_op jit(solution)/shard_map/all_to_all | solution.py:480
  67.3 1.2 %final.1 = f32[6,64,512]{2,1,0:T(8,128)} custom-call(f32[6,64,512]{2,1,0:T(8,128)S(1)} %get-tuple-element.33.fine_ref, f32[2,64,128]{2,1,0:T(8,128)S(1)} %get-tuple-element.41.edge_ref, f32[128,128]{1,0:T(8,128)S(1)} %bitcast.10), custom_call_target="tpu_custom_call" | custom-call | tf_op jit(solution)/shard_map/final/pallas_call | solution.py:446
Async XLA Ops:
  1.2 11.8 %collective-permute-start = (f32[6,4,512]{2,1,0:T(4,128)S(1)}, f32[6,4,512]{2,1,0:T(4,128)S(1)}, u32[]{:S(2)}, u32[]{:S(2)}) collective-permute-start(f32[6,4,512]{2,1,0:T(4,128)S(1)} %get-tuple-element.29), channel_id=1, source_target_pairs={{0,1},{2,3},{1,0},{3,2},{4,5},{6,7},{5,4},{7,6},{8,9},{10,11},{9,8... | collective-permute-start | bytes 147464 | tf_op jit(solution)/shard_map/ppermute | solution.py:465
  4.3 9.2 %collective-permute-start.1 = (f32[6,4,512]{2,1,0:T(4,128)S(1)}, f32[6,4,512]{2,1,0:T(4,128)S(1)}, u32[]{:S(2)}, u32[]{:S(2)}) collective-permute-start(f32[6,4,512]{2,1,0:T(4,128)S(1)} %get-tuple-element.30), channel_id=1, source_target_pairs={{1,2},{2,1},{5,6},{6,5},{9,10},{10,9},{13,14},{14,13},{17,18},{18,... | collective-permute-start | bytes 147464 | tf_op jit(solution)/shard_map/ppermute | solution.py:465
  13.6 5.4 %collective-permute-start.2 = (f32[72,128]{1,0:T(8,128)S(1)}, f32[72,128]{1,0:T(8,128)S(1)}, u32[]{:S(2)}, u32[]{:S(2)}) collective-permute-start(f32[72,128]{1,0:T(8,128)S(1)} %get-tuple-element.38), channel_id=1, source_target_pairs={{0,4},{8,12},{4,0},{12,8},{1,5},{9,13},{5,1},{13,9},{2,6},{10,14},... | collective-permute-start | bytes 110600 | tf_op jit(solution)/shard_map/ppermute | solution.py:465
  15.6 3.5 %collective-permute-start.3 = (f32[72,128]{1,0:T(8,128)S(1)}, f32[72,128]{1,0:T(8,128)S(1)}, u32[]{:S(2)}, u32[]{:S(2)}) collective-permute-start(f32[72,128]{1,0:T(8,128)S(1)} %get-tuple-element.39), channel_id=1, source_target_pairs={{4,8},{8,4},{5,9},{9,5},{6,10},{10,6},{7,11},{11,7},{20,24},{24,20... | collective-permute-start | bytes 110600 | tf_op jit(solution)/shard_map/ppermute | solution.py:465

commit v4 on v3

--- a/solution.py
+++ b/solution.py
@@ -11,8 +11,8 @@
 STEP = 0.24
 FACE = 0.24 * 0.25 * 0.25
 F32, BF16 = jnp.float32, jnp.bfloat16
-TOP = 16
-BUF = 96
+TOP = 8
+BUF = 88
 PARAMS = pltpu.CompilerParams(vmem_limit_bytes=24 << 20)
 VMEM = pl.BlockSpec(memory_space=pltpu.VMEM)
 SMEM = pl.BlockSpec(memory_space=pltpu.SMEM)
@@ -23,10 +23,13 @@
     return lax.broadcasted_iota(jnp.int32, shape, len(shape) - 1)
 
 
-def put_pair(packed_ref, k, low, high):
+SLOT, BACK = 21, 3
+
+
+def put_pair(packed_ref, k, low, high, height=SLOT):
     left = lanes(low.shape) < 64
-    packed_ref[pl.ds(k, 16, stride=48), :] = jnp.where(left, low, pltpu.roll(high, 64, 1))
-    packed_ref[pl.ds(24 + k, 16, stride=48), :] = jnp.where(left, pltpu.roll(low, 64, 1), high)
+    packed_ref[pl.ds(k, 16, stride=2 * height), :] = jnp.where(left, low, pltpu.roll(high, 64, 1))
+    packed_ref[pl.ds(height + k, 16, stride=2 * height), :] = jnp.where(left, pltpu.roll(low, 64, 1), high)
 
 
 def split_dot(x, matrix, transposed=False):
@@ -68,10 +71,12 @@
         strips_ref[tile, rows : rows + count, :] = total
 
 
-def load_kernel(nu_hbm, starts_ref, state_ref, pair_ref, cross_ref, consts_ref, weights_ref, order_ref, spread_ref, nu_ref, sems):
+def load_kernel(nu_hbm, starts_ref, map_ref, state_ref, entries_ref, pair_ref, cross_ref, consts_ref, weights_ref, order_ref,
+                spread_ref, nu_ref, sems):
     outer = [pl.ds(0, 8), pl.ds(56, 8), pl.ds(8, 48)]
     copies = [pltpu.make_async_copy(starts_ref.at[:, r, :], state_ref.at[:, r, :], sems.at[i]) for i, r in enumerate(outer)]
     copies.append(pltpu.make_async_copy(nu_hbm, nu_ref, sems.at[3]))
+    copies.append(pltpu.make_async_copy(map_ref, entries_ref, sems.at[4]))
     for copy in copies:
         copy.start()
     row, column = lax.axis_index("row"), lax.axis_index("gz")
@@ -86,7 +91,8 @@
     to = jnp.where((at >= 4) & (at < 8), base, jnp.where((at >= 20) & (at < 24), base + 63, -1))
     to = jnp.where(field < 6, to, -1)
     spread_ref[...] = jnp.where(to == target, F32(1.0 / 16.0), F32(0.0)).astype(BF16)
-    radius = (lax.broadcasted_iota(jnp.int32, (BUF, 128), 0) - TOP + row * 64).astype(F32)
+    line = lax.broadcasted_iota(jnp.int32, (BUF, 128), 0)
+    radius = (jnp.where(line >= TOP + 68, line - (TOP + 72), line - TOP) + row * 64).astype(F32)
     weights_ref[0] = (radius + 1.0) / (radius + 0.5)
     weights_ref[1] = radius / (radius + 0.5)
     copies[3].wait()
@@ -100,6 +106,7 @@
     values = [flag(row % 2 == 1), flag(column % 2 == 1), flag(row > 0), flag(row < 3)]
     values += [flag((at >= low) & (at < high)), rates((0, 1, 2, 3)), rates((4, 5, 5, 5)), rates((1, 1, 1, 1))]
     values += [rates((f, f, f, f)) for f in range(6)]
+    values += [flag(lax.axis_index("tm") > 0)]
     total = jnp.zeros((16, 128), F32)
     for r, value in enumerate(values):
         total = jnp.where(line == r, value, total)
@@ -112,14 +119,16 @@
         pair_ref[f] = jnp.where(odd, first, last)
         cross_ref[f] = jnp.where(odd, last, first)
     copies[2].wait()
-
-
-def load(diffusivity, state):
+    copies[4].wait()
+
+
+def load(diffusivity, state, coarse_map):
     shape = lambda *dims: jax.ShapeDtypeStruct(dims, F32)
     return pl.pallas_call(
         load_kernel,
         out_shape=(
             shape(6, 64, 512),
+            shape(36, 16, 128),
             shape(6, 4, 512),
             shape(6, 4, 512),
             shape(16, 128),
@@ -127,17 +136,15 @@
             jax.ShapeDtypeStruct((512, 512), BF16),
             jax.ShapeDtypeStruct((256, 384), BF16),
         ),
-        in_specs=[HBM, HBM],
-        out_specs=(VMEM,) * 7,
-        scratch_shapes=[pltpu.SMEM((6,), F32), pltpu.SemaphoreType.DMA((4,))],
+        in_specs=[HBM] * 3,
+        out_specs=(VMEM,) * 8,
+        scratch_shapes=[pltpu.SMEM((6,), F32), pltpu.SemaphoreType.DMA((5,))],
         compiler_params=PARAMS,
         name="load",
-    )(diffusivity, state)
-
-
-def prep_kernel(consts_ref, order_ref, state_ref, map_ref, cells_ref, packed_ref, pair_ref, cross_ref, strips_ref, entries, sem):
-    map_copy = pltpu.make_async_copy(map_ref, entries, sem)
-    map_copy.start()
+    )(diffusivity, state, coarse_map)
+
+
+def prep_kernel(consts_ref, order_ref, state_ref, entries_ref, cells_ref, packed_ref, drift_ref, pair_ref, cross_ref, strips_ref):
     piece = lambda f, t: state_ref[f, :, 128 * t : 128 * t + 128]
     odd = jnp.broadcast_to(const(consts_ref, 1), (64, 128)) > 0.5
     right, left = messages(piece, 64)
@@ -148,14 +155,18 @@
     for f in range(6):
         for k in range(4):
             cells_ref[f, k] = ordered[64 * f : 64 * f + 64, 128 * k : 128 * k + 128]
-    put_means(packed_ref, 21, lambda f, k, r: cells_ref[f, k, pl.ds(r, 16, stride=4), :], False)
-    map_copy.wait()
+    means = block_means(lambda f, k, r: cells_ref[f, k, pl.ds(r, 16, stride=4), :], False)
+    later = jnp.broadcast_to(const(consts_ref, 14), (16, 128)) > 0.5
+    for f in range(6):
+        terms = [entries_ref[6 * f + g] * means[g] for g in range(6)]
+        total = (terms[0] + terms[1]) + (terms[2] + terms[3]) + (terms[4] + terms[5])
+        drift_ref[f] = jnp.where(later, total, F32(0.0))
     for f in range(6):
         for j in range(3):
-            put_pair(packed_ref, 3 * f + j, entries[6 * f + j], entries[6 * f + j + 3])
-
-
-def put_means(packed_ref, at, load, inner):
+            put_pair(packed_ref, 3 * f + j, entries_ref[6 * f + j], entries_ref[6 * f + j + 3])
+
+
+def block_means(load, inner):
     means = []
     for f in range(6):
         total = jnp.zeros((16, 128), F32)
@@ -165,22 +176,27 @@
             lane = lanes((16, 128))
             total = jnp.where((lane > 0) & (lane < 127), total, F32(0.0))
         means.append(total * F32(1.0 / 16.0))
-    for j in range(3):
-        put_pair(packed_ref, at + j, means[j], means[j + 3])
-
-
-def prep(consts, order, state, coarse_map):
+    return means
+
+
+def prep(consts, order, state, entries):
     shape = lambda *dims: jax.ShapeDtypeStruct(dims, F32)
     return pl.pallas_call(
         prep_kernel,
-        out_shape=(shape(6, 4, 64, 128), shape(768, 128), shape(72, 128), shape(72, 128), shape(3, 72, 128)),
-        in_specs=[VMEM, VMEM, VMEM, HBM],
-        out_specs=(VMEM,) * 5,
-        scratch_shapes=[pltpu.VMEM((36, 16, 128), F32), pltpu.SemaphoreType.DMA(())],
+        out_shape=(
+            shape(6, 4, 64, 128),
+            shape(32 * SLOT, 128),
+            shape(6, 16, 128),
+            shape(72, 128),
+            shape(72, 128),
+            shape(3, 72, 128),
+        ),
+        in_specs=[VMEM] * 4,
+        out_specs=(VMEM,) * 6,
         compiler_params=PARAMS,
         cost_estimate=pl.CostEstimate(flops=4_000_000, bytes_accessed=2_000_000, transcendentals=0),
         name="prep",
-    )(consts, order, state, coarse_map)
+    )(consts, order, state, entries)
 
 
 def const(consts_ref, r):
@@ -218,14 +234,19 @@
     )(consts, pair_rows, cross_rows, pair_columns, cross_columns)
 
 
-def middle_kernel(consts_ref, weights_ref, order_ref, cells_ref, pair_rows_ref, cross_rows_ref, packed_in,
-                  strips_in, fine_ref, packed_ref, strips_ref, buffer, face, halo, flat):
+def halo_exists(consts_ref):
+    full = lambda r: jnp.broadcast_to(const(consts_ref, r), (8, 128))
+    return jnp.where(lax.broadcasted_iota(jnp.int32, (8, 128), 0) < 4, full(3), full(2)) > 0.5
+
+
+def middle_kernel(consts_ref, weights_ref, order_ref, cells_ref, drift_ref, pair_rows_ref, cross_rows_ref,
+                  packed_in, strips_in, fine_ref, packed_ref, strips_ref, own_ref, buffer, face, halo, flat):
     del packed_in, strips_in
     above, below = strips_above_below(consts_ref, pair_rows_ref, cross_rows_ref)
     for f in range(6):
         for t in range(4):
-            halo[8 * f : 8 * f + 4, 128 * t : 128 * t + 128] = above(f, t)
-            halo[8 * f + 4 : 8 * f + 8, 128 * t : 128 * t + 128] = below(f, t)
+            halo[8 * f : 8 * f + 4, 128 * t : 128 * t + 128] = below(f, t)
+            halo[8 * f + 4 : 8 * f + 8, 128 * t : 128 * t + 128] = above(f, t)
     put_strips(strips_ref, 64, below, 4)
     put_strips(strips_ref, 68, above, 4)
     ordered = split_dot(halo[...], order_ref[...])
@@ -233,10 +254,10 @@
         for k in range(4):
             buffer[0, f, k, TOP : TOP + 64, :] = cells_ref[f, k]
             piece = ordered[8 * f : 8 * f + 8, 128 * k : 128 * k + 128]
-            buffer[0, f, k, TOP - 4 : TOP, :] = piece[0:4]
-            buffer[0, f, k, TOP + 64 : TOP + 68, :] = piece[4:8]
-    has_above = jnp.broadcast_to(const(consts_ref, 2), (8, 128)) > 0.5
-    has_below = jnp.broadcast_to(const(consts_ref, 3), (8, 128)) > 0.5
+            buffer[0, f, k, TOP + 64 : TOP + 72, :] = piece
+            buffer[0, f, k, TOP - 1 : TOP, :] = piece[7:8]
+            buffer[0, f, k, TOP + 72 : TOP + 73, :] = cells_ref[f, k, 0:1, :]
+    exists = halo_exists(consts_ref)
 
     def step_cells(now, later, tiles, last):
         for i in tiles:
@@ -263,10 +284,11 @@
                         (east[k] * (rate - face[k + 1, rows, :]) + west[k] * (rate + face[k, rows, :]))
                         + center[k] * (keep + face[5 + k, rows, :])
                     )
-                    if i == 1:
-                        new = jnp.where(has_above, new, F32(0.0))
-                    if i == 10:
-                        new = jnp.where(has_below, new, F32(0.0))
+                    if i == 9:
+                        new = jnp.where(exists, new, F32(0.0))
+                        buffer[later, f, k, TOP - 1 : TOP, :] = new[7:8]
+                    if i == 1 and not last:
+                        buffer[later, f, k, TOP + 72 : TOP + 73, :] = new[0:1]
                     buffer[later, f, k, rows, :] = new
                     if last:
                         at = 64 * f + 8 * i - TOP
@@ -274,77 +296,80 @@
 
     for step in range(FSTEPS):
         last = step == FSTEPS - 1
-        step_cells(step % 2, (step + 1) % 2, range(2, 10) if last else range(1, 11), last)
+        step_cells(step % 2, (step + 1) % 2, range(1, 9) if last else range(1, 10), last)
     slot = FSTEPS % 2
-    put_means(packed_ref, 18, lambda f, k, r: buffer[slot, f, k, pl.ds(TOP + r, 16, stride=4), :], True)
+    means = block_means(lambda f, k, r: buffer[slot, f, k, pl.ds(TOP + r, 16, stride=4), :], True)
+    for j in range(3):
+        put_pair(own_ref, j, means[j], means[j + 3], BACK)
+        put_pair(packed_ref, 18 + j, means[j] - drift_ref[j], means[j + 3] - drift_ref[j + 3])
     fine_ref[...] = split_dot(flat[...], order_ref[...], transposed=True).reshape(6, 64, 512)
 
 
-def middle(consts, weights, order, cells, pair_rows, cross_rows, packed, strips):
+def middle(consts, weights, order, cells, drift, pair_rows, cross_rows, packed, strips):
     return pl.pallas_call(
         middle_kernel,
         out_shape=(
             jax.ShapeDtypeStruct((6, 64, 512), F32),
-            jax.ShapeDtypeStruct((768, 128), F32),
+            jax.ShapeDtypeStruct((32 * SLOT, 128), F32),
             jax.ShapeDtypeStruct((3, 72, 128), F32),
+            jax.ShapeDtypeStruct((32 * BACK, 128), F32),
         ),
-        in_specs=[VMEM] * 8,
-        out_specs=(VMEM,) * 3,
+        in_specs=[VMEM] * 9,
+        out_specs=(VMEM,) * 4,
         scratch_shapes=[
             pltpu.VMEM((2, 6, 4, BUF, 128), F32),
             pltpu.VMEM((9, BUF, 128), F32),
             pltpu.VMEM((48, 512), F32),
             pltpu.VMEM((384, 512), F32),
         ],
-        input_output_aliases={6: 1, 7: 2},
+        input_output_aliases={7: 1, 8: 2},
         compiler_params=PARAMS,
         cost_estimate=pl.CostEstimate(flops=20_000_000, bytes_accessed=4_000_000, transcendentals=200_000),
         name="middle",
-    )(consts, weights, order, cells, pair_rows, cross_rows, packed, strips)
-
-
-def sides_kernel(consts_ref, weights_ref, spread_ref, strips_ref, pair_ref, cross_ref, packed_in,
-                 edge_ref, packed_ref, buffer, face):
+    )(consts, weights, order, cells, drift, pair_rows, cross_rows, packed, strips)
+
+
+def sides_kernel(consts_ref, weights_ref, spread_ref, strips_ref, pair_ref, cross_ref, packed_in, own_in,
+                 edge_ref, packed_ref, own_ref, buffer):
     full = lambda r, count=8: jnp.broadcast_to(const(consts_ref, r), (count, 128))
-    for source, target, count in ((0, TOP, 64), (64, TOP + 64, 4), (68, TOP - 4, 4)):
-        at = lanes((count, 128)) % 32
-        odd = full(1, count) > 0.5
-        pair, cross = pair_ref[source : source + count, :], cross_ref[source : source + count, :]
-        from_left, from_right = jnp.where(odd, pair, cross), jnp.where(odd, cross, pair)
-        for tile in range(3):
-            value = jnp.where(at < 4, moved(from_left, -4 * tile), strips_ref[tile, source : source + count, :])
-            value = jnp.where((at >= 24) & (at < 28), moved(from_right, 4 * tile), value)
-            buffer[0, tile, target : target + count, :] = value
-    has_above, has_below, inside = full(2) > 0.5, full(3) > 0.5, full(4) > 0.5
+    at = lanes((72, 128)) % 32
+    odd = full(1, 72) > 0.5
+    pair, cross = pair_ref[...], cross_ref[...]
+    from_left, from_right = jnp.where(odd, pair, cross), jnp.where(odd, cross, pair)
+    for tile in (2, 1, 0):
+        value = jnp.where(at < 4, moved(from_left, -4 * tile), strips_ref[tile])
+        value = jnp.where((at >= 24) & (at < 28), moved(from_right, 4 * tile), value)
+        buffer[0, tile, TOP : TOP + 72, :] = value
+        buffer[0, tile, TOP - 1 : TOP, :] = value[71:72]
+        buffer[0, tile, TOP + 72 : TOP + 73, :] = value[0:1]
+    exists, inside = halo_exists(consts_ref), full(4) > 0.5
     rates = [full(5 + tile) for tile in range(3)]
     keeps = [1.0 - 4.0 * rate for rate in rates]
     for step in range(FSTEPS):
         now, later = step % 2, (step + 1) % 2
         last = step == FSTEPS - 1
-        tiles = range(2, 10) if last else range(1, 11)
-        for i in tiles:
-            rows = pl.ds(8 * i, 8)
-            speed = FACE * jnp.tanh(buffer[now, 2, rows, :])
-            face[0, rows, :] = speed + pltpu.roll(speed, 127, 1)
-            face[1, rows, :] = speed + pltpu.roll(speed, 1, 1)
-        for i in tiles:
+        for i in range(1, 9) if last else range(1, 10):
             rows = pl.ds(8 * i, 8)
             up, down = weights_ref[0, rows, :], weights_ref[1, rows, :]
-            fe, fw = face[0, rows, :], face[1, rows, :]
+            center = [buffer[now, tile, rows, :] for tile in range(3)]
+            east = [pltpu.roll(c, 127, 1) for c in center]
+            west = [pltpu.roll(c, 1, 1) for c in center]
+            speed = jnp.tanh(center[2])
+            fe, fw = FACE * (speed + jnp.tanh(east[2])), FACE * (speed + jnp.tanh(west[2]))
             for tile in range(2 if last else 3):
                 rate = rates[tile]
-                center = buffer[now, tile, rows, :]
                 north = buffer[now, tile, pl.ds(8 * i + 1, 8), :]
                 south = buffer[now, tile, pl.ds(8 * i - 1, 8), :]
                 new = rate * (up * north + down * south) + (
-                    (pltpu.roll(center, 127, 1) * (rate - fe) + pltpu.roll(center, 1, 1) * (rate + fw))
-                    + center * (keeps[tile] + (fw - fe))
+                    (east[tile] * (rate - fe) + west[tile] * (rate + fw)) + center[tile] * (keeps[tile] + (fw - fe))
                 )
-                if i == 1:
-                    new = jnp.where(has_above, new, F32(0.0))
-                if i == 10:
-                    new = jnp.where(has_below, new, F32(0.0))
+                if i == 9:
+                    new = jnp.where(exists, new, F32(0.0))
                 new = jnp.where(inside, new, F32(0.0))
+                if i == 9:
+                    buffer[later, tile, TOP - 1 : TOP, :] = new[7:8]
+                if i == 1 and not last:
+                    buffer[later, tile, TOP + 72 : TOP + 73, :] = new[0:1]
                 buffer[later, tile, rows, :] = new
                 if last:
                     edge_ref[tile, 8 * i - TOP : 8 * i - TOP + 8, :] = new
@@ -357,63 +382,69 @@
     left = lanes((16, 128)) % 64 == 0
     for j in range(3):
         piece = own[:, 128 * j : 128 * j + 128]
-        even, odd = pl.ds(18 + j, 16, stride=48), pl.ds(42 + j, 16, stride=48)
-        packed_ref[even, :] = packed_in[even, :] + jnp.where(left, piece, F32(0.0))
-        packed_ref[odd, :] = packed_in[odd, :] + jnp.where(left, F32(0.0), piece)
-
-
-def sides(consts, weights, spread, strips, pair_columns, cross_columns, packed):
+        pieces = jnp.where(left, piece, F32(0.0)), jnp.where(left, F32(0.0), piece)
+        for half in range(2):
+            rows = pl.ds(SLOT * half + 18 + j, 16, stride=2 * SLOT)
+            packed_ref[rows, :] = packed_in[rows, :] + pieces[half]
+            rows = pl.ds(BACK * half + j, 16, stride=2 * BACK)
+            own_ref[rows, :] = own_in[rows, :] + pieces[half]
+
+
+def sides(consts, weights, spread, strips, pair_columns, cross_columns, packed, own):
     return pl.pallas_call(
         sides_kernel,
-        out_shape=(jax.ShapeDtypeStruct((2, 64, 128), F32), jax.ShapeDtypeStruct((768, 128), F32)),
-        in_specs=[VMEM] * 7,
-        out_specs=(VMEM, VMEM),
-        scratch_shapes=[pltpu.VMEM((2, 3, BUF, 128), F32), pltpu.VMEM((2, BUF, 128), F32)],
-        input_output_aliases={6: 1},
+        out_shape=(
+            jax.ShapeDtypeStruct((2, 64, 128), F32),
+            jax.ShapeDtypeStruct((32 * SLOT, 128), F32),
+            jax.ShapeDtypeStruct((32 * BACK, 128), F32),
+        ),
+        in_specs=[VMEM] * 8,
+        out_specs=(VMEM,) * 3,
+        scratch_shapes=[pltpu.VMEM((2, 3, BUF, 128), F32)],
+        input_output_aliases={6: 1, 7: 2},
         compiler_params=PARAMS,
         name="sides",
-    )(consts, weights, spread, strips, pair_columns, cross_columns, packed)
+    )(consts, weights, spread, strips, pair_columns, cross_columns, packed, own)
 
 
 def scan_kernel(slices, packed_ref, mapped_ref, other, rows):
     other[...] = pltpu.roll(packed_ref[...], 64, 1)
     carry = [jnp.zeros((1, 128), F32)] * 6
     for n in range(slices):
-        base = 24 * n
+        base = SLOT * n
         line = lambda k, half: (other if half else packed_ref)[pl.ds(base + k, 1), :]
         mapped = []
         for f in range(6):
             terms = [line(3 * f + g % 3, g >= 3) * carry[g] for g in range(6)]
             total = (terms[0] + terms[1]) + (terms[2] + terms[3]) + (terms[4] + terms[5])
-            rows[f, pl.ds(n, 1), :] = total
-            mapped.append(total)
-        if n < slices - 1:
-            carry = [mapped[f] + (line(18 + f % 3, f >= 3) - line(45 + f % 3, f >= 3)) for f in range(6)]
+            mapped.append(total + line(18 + f % 3, f >= 3))
+            rows[f, pl.ds(n, 1), :] = mapped[f]
+        carry = mapped
     left = lanes((slices, 128)) < 64
     for j in range(3):
-        mapped_ref[pl.ds(j, slices, stride=4), :] = jnp.where(left, rows[j], pltpu.roll(rows[j + 3], 64, 1))
+        mapped_ref[pl.ds(j, slices, stride=BACK), :] = jnp.where(left, rows[j], pltpu.roll(rows[j + 3], 64, 1))
 
 
 def scanned(packed, slices):
     return pl.pallas_call(
         functools.partial(scan_kernel, slices),
-        out_shape=jax.ShapeDtypeStruct((4 * slices, 128), F32),
+        out_shape=jax.ShapeDtypeStruct((BACK * slices, 128), F32),
         in_specs=[VMEM],
         out_specs=VMEM,
-        scratch_shapes=[pltpu.VMEM((24 * slices, 128), F32), pltpu.VMEM((6, slices, 128), F32)],
+        scratch_shapes=[pltpu.VMEM((SLOT * slices, 128), F32), pltpu.VMEM((6, slices, 128), F32)],
         compiler_params=PARAMS,
         name="scan",
     )(packed)
 
 
-def final_kernel(fine_ref, edge_ref, mapped_ref, out_ref, wide, done, sems):
+def final_kernel(fine_ref, edge_ref, own_ref, mapped_ref, out_ref, wide, done, sems):
     left = lanes((16, 128)) < 64
     upper = lax.broadcasted_iota(jnp.int32, (8, 128), 0) < 4
     lane = lanes((8, 128))
     for f in range(6):
         j = f % 3
-        even = mapped_ref[pl.ds(j, 16, stride=8), :]
-        odd = mapped_ref[pl.ds(4 + j, 16, stride=8), :]
+        rows = pl.ds(j, 16, stride=2 * BACK), pl.ds(BACK + j, 16, stride=2 * BACK)
+        even, odd = (mapped_ref[r, :] - own_ref[r, :] for r in rows)
         if f < 3:
             cells = jnp.where(left, even, pltpu.roll(odd, 64, 1))
         else:
@@ -442,11 +473,11 @@
         copy.wait()
 
 
-def final(fine_state, edge, mapped):
+def final(fine_state, edge, own, mapped):
     return pl.pallas_call(
         final_kernel,
         out_shape=jax.ShapeDtypeStruct((6, 64, 512), F32),
-        in_specs=[VMEM] * 3,
+        in_specs=[VMEM] * 4,
         out_specs=HBM,
         scratch_shapes=[
             pltpu.VMEM((6, 4, 16, 128), F32),
@@ -455,7 +486,7 @@
         ],
         compiler_params=PARAMS,
         name="final",
-    )(fine_state, edge, mapped)
+    )(fine_state, edge, own, mapped)
 
 
 def swapped(pair, cross, axis):
@@ -468,17 +499,23 @@
 def local(starts, coarse_map, diffusivity):
     in_hbm = lambda x: pltpu.with_memory_space_constraint(x, pltpu.HBM)
     slices = lax.axis_size("tm")
-    state, pair_rows, cross_rows, consts, weights, order, spread = load(in_hbm(diffusivity), in_hbm(starts[0]))
+    state, entries, pair_rows, cross_rows, consts, weights, order, spread = load(
+        in_hbm(diffusivity), in_hbm(starts[0]), in_hbm(coarse_map[0])
+    )
     pair_rows, cross_rows = swapped(pair_rows, cross_rows, "row")
-    cells, packed, pair_columns, cross_columns, strips = prep(consts, order, state, in_hbm(coarse_map[0]))
+    cells, packed, drift, pair_columns, cross_columns, strips = prep(consts, order, state, entries)
     pair_columns, cross_columns = corners(consts, pair_rows, cross_rows, pair_columns, cross_columns)
     pair_columns, cross_columns = swapped(pair_columns, cross_columns, "gz")
-    fine_state, packed, strips = middle(consts, weights, order, cells, pair_rows, cross_rows, packed, strips)
-    edge, packed = sides(consts, weights, spread, strips, pair_columns, cross_columns, packed)
-    packed = lax.all_to_all(packed, "tm", 0, 0, tiled=True)
+    fine_state, packed, strips, own = middle(
+        consts, weights, order, cells, drift, pair_rows, cross_rows, packed, strips
+    )
+    edge, packed, own = sides(consts, weights, spread, strips, pair_columns, cross_columns, packed, own)
+    slots = packed.reshape(slices, 1, SLOT * 128)
+    packed = lax.all_to_all(slots, "tm", 0, 0, tiled=True).reshape(packed.shape)
     mapped = scanned(packed, slices)
-    mapped = lax.all_to_all(mapped, "tm", 0, 0, tiled=True)
-    return final(fine_state, edge, mapped)[None]
+    slots = mapped.reshape(slices, 1, BACK * 128)
+    mapped = lax.all_to_all(slots, "tm", 0, 0, tiled=True).reshape(mapped.shape)
+    return final(fine_state, edge, own, mapped)[None]
 
 
 def solution(mesh):

time: 68.8 us -> 67.2 us (0.977)
  Pallas kernels: 8.09 us -> 6.78 us
  blocking collectives: 47 us -> 45.9 us
  waiting for transfers between devices: 0.46 us -> 1.41 us
    all_to_all x2, blocking collectives: 47 us -> 45.9 us  [the longest x1 27.3 us: local(): packed = lax.all_to_all(slots, 'tm', 0, 0, tiled=True).reshape(packed.shape)]
    ppermute x2, waiting for transfers between devices: 0.46 us -> 1.4 us  [swapped(): lax.ppermute(cross, axis, both(couples(1)))]
    pallas_call x2, Pallas kernels: 2.79 us -> 1.92 us  [the longest x1 1.29 us: load(): pl.pallas_call(load_kernel, out_shape=(shape(6, 64, 512), shape(36, 16, 1...]
  transfers between devices with their start and end apart: 4 -> 4, of which waited for: 1 -> 1; matrix products, arithmetic and copies ran while one was open for 0% -> 0% of each run, Pallas kernels for 6% -> 5%
where the time goes in v4:
time: 67.2 us; the launch traced here: 67 us
  blocking collectives  45.9 us (68%)
  starting transfers between devices  12.8 us (19%)
  Pallas kernels  6.78 us (10%)
  waiting for transfers between devices  1.41 us (2%)
    all_to_all x1, blocking collectives, local(): packed = lax.all_to_all(slots, 'tm', 0, 0, tiled=True).reshape(packed.shape)  27.3 us
    all_to_all x1, blocking collectives, local(): mapped = lax.all_to_all(slots, 'tm', 0, 0, tiled=True).reshape(mapped.shape)  18.5 us
    ppermute x2, starting transfers between devices, swapped(): lax.ppermute(cross, axis, both(couples(1)))  7.79 us
    ppermute x2, starting transfers between devices, swapped(): lax.ppermute(pair, axis, both(couples(0)))  5.03 us
    pallas_call x1, Pallas kernels, middle(): pl.pallas_call(middle_kernel, out_shape=(jax.ShapeDtypeStruct((6, 64, 512...  2.45 us
    ppermute x2, waiting for transfers between devices, swapped(): lax.ppermute(cross, axis, both(couples(1)))  1.4 us
  transfers between devices with their start and end apart: 4, of which 1 were waited for; matrix products, arithmetic and copies ran while one was open for 0% of the time, Pallas kernels for 5%

profile of v4, /device:TPU:4, one launch (start us, length us, event | category | flops | bytes accessed | tf_op | source)
XLA Modules:
  0.0 67.0 jit_solution(11706481788117019128)
XLA Ops:
  0.0 1.3 %load.1 = (f32[6,64,512]{2,1,0:T(8,128)S(1)}, f32[36,16,128]{2,1,0:T(8,128)S(1)}, f32[6,4,512]{2,1,0:T(4,128)S(1)}, f32[6,4,512]{2,1,0:T(4,128)S(1)}, f32[16,128...) custom-call(f32[6]{0:T(128)} %nu_hbm.1, ...), custom_call_target="tpu_custom_call" | custom-call | tf_op jit(solution)/shard_map/load/pallas_call | solution.py:127
  1.3 3.1 %collective-permute-start = (f32[6,4,512]{2,1,0:T(4,128)S(1)}, f32[6,4,512]{2,1,0:T(4,128)S(1)}, u32[]{:S(2)}, u32[]{:S(2)}) collective-permute-start(f32[6,4,512]{2,1,0:T(4,128)S(1)} %get-tuple-element.35), channel_id=1, source_target_pairs={{0,1},{2,3},{1,0},{3,2},{4,5},{6,7},{5,4},{7,6},{8,9},{10,11},{9,8... | collective-permute-start | bytes 147464 | tf_op jit(solution)/shard_map/ppermute | solution.py:496
  4.4 7.1 %collective-permute-start.1 = (f32[6,4,512]{2,1,0:T(4,128)S(1)}, f32[6,4,512]{2,1,0:T(4,128)S(1)}, u32[]{:S(2)}, u32[]{:S(2)}) collective-permute-start(f32[6,4,512]{2,1,0:T(4,128)S(1)} %get-tuple-element.36), channel_id=1, source_target_pairs={{1,2},{2,1},{5,6},{6,5},{9,10},{10,9},{13,14},{14,13},{17,18},{18,... | collective-permute-start | bytes 147464 | tf_op jit(solution)/shard_map/ppermute | solution.py:496
  11.5 0.6 prep.1
  12.2 0.0 collective-permute-done.pair_rows_ref
  12.2 1.4 %collective-permute-done.1.cross_rows_ref = f32[6,4,512]{2,1,0:T(4,128)S(1)} collective-permute-done((f32[6,4,512]{2,1,0:T(4,128)S(1)}, f32[6,4,512]{2,1,0:T(4,128)S(1)}, u32[]{:S(2)}, u32[]{:S(2)}) %collective-permute-start.1) | collective-permute-done | bytes 49184 | tf_op jit(solution)/shard_map/ppermute | solution.py:496
  13.6 0.1 corners.1
  13.7 1.9 %collective-permute-start.2 = (f32[72,128]{1,0:T(8,128)S(1)}, f32[72,128]{1,0:T(8,128)S(1)}, u32[]{:S(2)}, u32[]{:S(2)}) collective-permute-start(f32[72,128]{1,0:T(8,128)S(1)} %get-tuple-element.44), channel_id=1, source_target_pairs={{0,4},{8,12},{4,0},{12,8},{1,5},{9,13},{5,1},{13,9},{2,6},{10,14},... | collective-permute-start | bytes 110600 | tf_op jit(solution)/shard_map/ppermute | solution.py:496
  15.6 0.7 collective-permute-start.3
  16.3 2.5 %middle.1 = (f32[6,64,512]{2,1,0:T(8,128)S(1)}, f32[672,128]{1,0:T(8,128)S(1)}, f32[3,72,128]{2,1,0:T(8,128)S(1)}, f32[96,128]{1,0:T(8,128)S(1)}) custom-call(f32[16,128]{1,0:T(8,128)S(1)} %get-tuple-element.28.consts_ref, f32[2,88,128]{2,1,0:T(8,128)S(1)} %get-tuple-element.29.weights_ref, ...), custom_call_target="tpu_custom_call", output_to_operand_aliasing={{1}: (7, {}), {2}: (8, {})} | custom-call | flops 20000000 | bytes 4000000 | tf_op jit(solution)/shard_map/middle/pallas_call | solution.py:309
  18.8 0.0 collective-permute-done.2.pair_ref
  18.8 0.0 collective-permute-done.3.cross_ref
  18.8 0.6 sides.1
  19.4 27.3 %all_to_all.10 = f32[32,1,2688]{2,1,0:T(1,128)S(1)} all-to-all(f32[32,1,2688]{2,1,0:T(1,128)S(1)} %bitcast.7), channel_id=1, replica_groups=mesh['tm'=32,'gz'=4,'row'=4] {'tm'}, dimensions={0} | all-to-all | bytes 688128 | tf_op jit(solution)/shard_map/all_to_all | solution.py:514
  46.8 0.5 scan.1
  47.2 18.5 %all_to_all.11 = f32[32,1,384]{2,1,0:T(1,128)S(1)} all-to-all(f32[32,1,384]{2,1,0:T(1,128)S(1)} %bitcast.9), channel_id=1, replica_groups=mesh['tm'=32,'gz'=4,'row'=4] {'tm'}, dimensions={0} | all-to-all | bytes 98304 | tf_op jit(solution)/shard_map/all_to_all | solution.py:517
  65.8 1.2 %final.1 = f32[6,64,512]{2,1,0:T(8,128)} custom-call(f32[6,64,512]{2,1,0:T(8,128)S(1)} %get-tuple-element.39.fine_ref, f32[2,64,128]{2,1,0:T(8,128)S(1)} %get-tuple-element.48.edge_ref, f32[96,128]{1,0:T(8,128)S(1)} %get-tuple-element.49.own_ref, f32[96,128]{1,0:T(8,128)S(1)} %bitcast.10), custom_call_target="tpu_custom_call" | custom-call | tf_op jit(solution)/shard_map/final/pallas_call | solution.py:477
Async XLA Ops:
  1.3 10.9 %collective-permute-start = (f32[6,4,512]{2,1,0:T(4,128)S(1)}, f32[6,4,512]{2,1,0:T(4,128)S(1)}, u32[]{:S(2)}, u32[]{:S(2)}) collective-permute-start(f32[6,4,512]{2,1,0:T(4,128)S(1)} %get-tuple-element.35), channel_id=1, source_target_pairs={{0,1},{2,3},{1,0},{3,2},{4,5},{6,7},{5,4},{7,6},{8,9},{10,11},{9,8... | collective-permute-start | bytes 147464 | tf_op jit(solution)/shard_map/ppermute | solution.py:496
  4.4 9.2 %collective-permute-start.1 = (f32[6,4,512]{2,1,0:T(4,128)S(1)}, f32[6,4,512]{2,1,0:T(4,128)S(1)}, u32[]{:S(2)}, u32[]{:S(2)}) collective-permute-start(f32[6,4,512]{2,1,0:T(4,128)S(1)} %get-tuple-element.36), channel_id=1, source_target_pairs={{1,2},{2,1},{5,6},{6,5},{9,10},{10,9},{13,14},{14,13},{17,18},{18,... | collective-permute-start | bytes 147464 | tf_op jit(solution)/shard_map/ppermute | solution.py:496
  13.7 5.1 %collective-permute-start.2 = (f32[72,128]{1,0:T(8,128)S(1)}, f32[72,128]{1,0:T(8,128)S(1)}, u32[]{:S(2)}, u32[]{:S(2)}) collective-permute-start(f32[72,128]{1,0:T(8,128)S(1)} %get-tuple-element.44), channel_id=1, source_target_pairs={{0,4},{8,12},{4,0},{12,8},{1,5},{9,13},{5,1},{13,9},{2,6},{10,14},... | collective-permute-start | bytes 110600 | tf_op jit(solution)/shard_map/ppermute | solution.py:496
  15.6 3.1 %collective-permute-start.3 = (f32[72,128]{1,0:T(8,128)S(1)}, f32[72,128]{1,0:T(8,128)S(1)}, u32[]{:S(2)}, u32[]{:S(2)}) collective-permute-start(f32[72,128]{1,0:T(8,128)S(1)} %get-tuple-element.45), channel_id=1, source_target_pairs={{4,8},{8,4},{5,9},{9,5},{6,10},{10,6},{7,11},{11,7},{20,24},{24,20... | collective-permute-start | bytes 110600 | tf_op jit(solution)/shard_map/ppermute | solution.py:496

commit v5 on v4

--- a/solution.py
+++ b/solution.py
@@ -6,6 +6,7 @@
 from jax.experimental import pallas as pl
 from jax.experimental.pallas import tpu as pltpu
 from jax.sharding import PartitionSpec as P
+
 
 FSTEPS = 4
 STEP = 0.24
@@ -493,10 +494,13 @@
     size = lax.axis_size(axis)
     couples = lambda first: [(i, i + 1) for i in range(first, size - 1, 2)]
     both = lambda links: links + [(b, a) for a, b in links]
+    if axis == "gz":
+        cross = lax.ppermute(cross, axis, both(couples(1)))
+        return lax.ppermute(pair, axis, both(couples(0))), cross
     return lax.ppermute(pair, axis, both(couples(0))), lax.ppermute(cross, axis, both(couples(1)))
 
 
-def local(starts, coarse_map, diffusivity):
+def whole(starts, coarse_map, diffusivity):
     in_hbm = lambda x: pltpu.with_memory_space_constraint(x, pltpu.HBM)
     slices = lax.axis_size("tm")
     state, entries, pair_rows, cross_rows, consts, weights, order, spread = load(
@@ -520,6 +524,4 @@
 
 def solution(mesh):
     placed = (P("tm", None, "row", "gz"), P("tm", None, "row", "gz"), P())
-    return jax.shard_map(
-        local, mesh=mesh, in_specs=placed, out_specs=P("tm", None, "row", "gz"), check_vma=False
-    )
+    return jax.shard_map(whole, mesh=mesh, in_specs=placed, out_specs=P("tm", None, "row", "gz"), check_vma=False)

time: 67.2 us -> 67.2 us (level)
    ppermute x0 -> x2, starting transfers between devices: none -> 2.58 us  [the longest x1 1.92 us: swapped(): return (lax.ppermute(pair, axis, both(couples(0))), cross)]
    ppermute x2 -> x1, starting transfers between devices: 5.03 us -> 3.11 us  [swapped(): lax.ppermute(pair, axis, both(couples(0)))]
    ppermute x2 -> x1, starting transfers between devices: 7.79 us -> 7.13 us  [swapped(): lax.ppermute(cross, axis, both(couples(1)))]
    ppermute x2 -> x1, waiting for transfers between devices: 1.4 us -> 1.4 us  [swapped(): lax.ppermute(cross, axis, both(couples(1)))]
where the time goes in v5:
time: 67.2 us; the launch traced here: 67 us
  blocking collectives  45.9 us (68%)
  starting transfers between devices  12.8 us (19%)
  Pallas kernels  6.78 us (10%)
  waiting for transfers between devices  1.41 us (2%)
    all_to_all x1, blocking collectives, whole(): packed = lax.all_to_all(slots, 'tm', 0, 0, tiled=True).reshape(packed.shape)  27.3 us
    all_to_all x1, blocking collectives, whole(): mapped = lax.all_to_all(slots, 'tm', 0, 0, tiled=True).reshape(mapped.shape)  18.5 us
    ppermute x1, starting transfers between devices, swapped(): lax.ppermute(cross, axis, both(couples(1)))  7.13 us
    ppermute x1, starting transfers between devices, swapped(): lax.ppermute(pair, axis, both(couples(0)))  3.11 us
    pallas_call x1, Pallas kernels, middle(): pl.pallas_call(middle_kernel, out_shape=(jax.ShapeDtypeStruct((6, 64, 512...  2.45 us
    ppermute x1, starting transfers between devices, swapped(): return (lax.ppermute(pair, axis, both(couples(0))), cross)  1.92 us
    ppermute x1, waiting for transfers between devices, swapped(): lax.ppermute(cross, axis, both(couples(1)))  1.4 us
  transfers between devices with their start and end apart: 4, of which 1 were waited for; matrix products, arithmetic and copies ran while one was open for 0% of the time, Pallas kernels for 5%

profile of v5, /device:TPU:4, one launch (start us, length us, event | category | flops | bytes accessed | tf_op | source)
XLA Modules:
  0.0 67.0 jit_solution(11706481788117019128)
XLA Ops:
  0.0 1.3 %load.1 = (f32[6,64,512]{2,1,0:T(8,128)S(1)}, f32[36,16,128]{2,1,0:T(8,128)S(1)}, f32[6,4,512]{2,1,0:T(4,128)S(1)}, f32[6,4,512]{2,1,0:T(4,128)S(1)}, f32[16,128...) custom-call(f32[6]{0:T(128)} %nu_hbm.1, ...), custom_call_target="tpu_custom_call" | custom-call | tf_op jit(solution)/shard_map/load/pallas_call | solution.py:128
  1.3 3.1 %collective-permute-start = (f32[6,4,512]{2,1,0:T(4,128)S(1)}, f32[6,4,512]{2,1,0:T(4,128)S(1)}, u32[]{:S(2)}, u32[]{:S(2)}) collective-permute-start(f32[6,4,512]{2,1,0:T(4,128)S(1)} %get-tuple-element.35), channel_id=1, source_target_pairs={{0,1},{2,3},{1,0},{3,2},{4,5},{6,7},{5,4},{7,6},{8,9},{10,11},{9,8... | collective-permute-start | bytes 147464 | tf_op jit(solution)/shard_map/ppermute | solution.py:500
  4.4 7.1 %collective-permute-start.1 = (f32[6,4,512]{2,1,0:T(4,128)S(1)}, f32[6,4,512]{2,1,0:T(4,128)S(1)}, u32[]{:S(2)}, u32[]{:S(2)}) collective-permute-start(f32[6,4,512]{2,1,0:T(4,128)S(1)} %get-tuple-element.36), channel_id=1, source_target_pairs={{1,2},{2,1},{5,6},{6,5},{9,10},{10,9},{13,14},{14,13},{17,18},{18,... | collective-permute-start | bytes 147464 | tf_op jit(solution)/shard_map/ppermute | solution.py:500
  11.5 0.6 prep.1
  12.2 0.0 collective-permute-done.pair_rows_ref
  12.2 1.4 %collective-permute-done.1.cross_rows_ref = f32[6,4,512]{2,1,0:T(4,128)S(1)} collective-permute-done((f32[6,4,512]{2,1,0:T(4,128)S(1)}, f32[6,4,512]{2,1,0:T(4,128)S(1)}, u32[]{:S(2)}, u32[]{:S(2)}) %collective-permute-start.1) | collective-permute-done | bytes 49184 | tf_op jit(solution)/shard_map/ppermute | solution.py:500
  13.6 0.1 corners.1
  13.7 1.9 %collective-permute-start.2 = (f32[72,128]{1,0:T(8,128)S(1)}, f32[72,128]{1,0:T(8,128)S(1)}, u32[]{:S(2)}, u32[]{:S(2)}) collective-permute-start(f32[72,128]{1,0:T(8,128)S(1)} %get-tuple-element.44), channel_id=1, source_target_pairs={{0,4},{8,12},{4,0},{12,8},{1,5},{9,13},{5,1},{13,9},{2,6},{10,14},... | collective-permute-start | bytes 110600 | tf_op jit(solution)/shard_map/ppermute | solution.py:499
  15.6 0.7 collective-permute-start.3
  16.3 2.5 %middle.1 = (f32[6,64,512]{2,1,0:T(8,128)S(1)}, f32[672,128]{1,0:T(8,128)S(1)}, f32[3,72,128]{2,1,0:T(8,128)S(1)}, f32[96,128]{1,0:T(8,128)S(1)}) custom-call(f32[16,128]{1,0:T(8,128)S(1)} %get-tuple-element.28.consts_ref, f32[2,88,128]{2,1,0:T(8,128)S(1)} %get-tuple-element.29.weights_ref, ...), custom_call_target="tpu_custom_call", output_to_operand_aliasing={{1}: (7, {}), {2}: (8, {})} | custom-call | flops 20000000 | bytes 4000000 | tf_op jit(solution)/shard_map/middle/pallas_call | solution.py:310
  18.8 0.0 collective-permute-done.2.pair_ref
  18.8 0.0 collective-permute-done.3.cross_ref
  18.8 0.6 sides.1
  19.4 27.3 %all_to_all.10 = f32[32,1,2688]{2,1,0:T(1,128)S(1)} all-to-all(f32[32,1,2688]{2,1,0:T(1,128)S(1)} %bitcast.7), channel_id=1, replica_groups=mesh['tm'=32,'gz'=4,'row'=4] {'tm'}, dimensions={0} | all-to-all | bytes 688128 | tf_op jit(solution)/shard_map/all_to_all | solution.py:518
  46.8 0.5 scan.1
  47.2 18.5 %all_to_all.11 = f32[32,1,384]{2,1,0:T(1,128)S(1)} all-to-all(f32[32,1,384]{2,1,0:T(1,128)S(1)} %bitcast.9), channel_id=1, replica_groups=mesh['tm'=32,'gz'=4,'row'=4] {'tm'}, dimensions={0} | all-to-all | bytes 98304 | tf_op jit(solution)/shard_map/all_to_all | solution.py:521
  65.8 1.2 %final.1 = f32[6,64,512]{2,1,0:T(8,128)} custom-call(f32[6,64,512]{2,1,0:T(8,128)S(1)} %get-tuple-element.39.fine_ref, f32[2,64,128]{2,1,0:T(8,128)S(1)} %get-tuple-element.48.edge_ref, f32[96,128]{1,0:T(8,128)S(1)} %get-tuple-element.49.own_ref, f32[96,128]{1,0:T(8,128)S(1)} %bitcast.10), custom_call_target="tpu_custom_call" | custom-call | tf_op jit(solution)/shard_map/final/pallas_call | solution.py:478
Async XLA Ops:
  1.3 10.9 %collective-permute-start = (f32[6,4,512]{2,1,0:T(4,128)S(1)}, f32[6,4,512]{2,1,0:T(4,128)S(1)}, u32[]{:S(2)}, u32[]{:S(2)}) collective-permute-start(f32[6,4,512]{2,1,0:T(4,128)S(1)} %get-tuple-element.35), channel_id=1, source_target_pairs={{0,1},{2,3},{1,0},{3,2},{4,5},{6,7},{5,4},{7,6},{8,9},{10,11},{9,8... | collective-permute-start | bytes 147464 | tf_op jit(solution)/shard_map/ppermute | solution.py:500
  4.4 9.2 %collective-permute-start.1 = (f32[6,4,512]{2,1,0:T(4,128)S(1)}, f32[6,4,512]{2,1,0:T(4,128)S(1)}, u32[]{:S(2)}, u32[]{:S(2)}) collective-permute-start(f32[6,4,512]{2,1,0:T(4,128)S(1)} %get-tuple-element.36), channel_id=1, source_target_pairs={{1,2},{2,1},{5,6},{6,5},{9,10},{10,9},{13,14},{14,13},{17,18},{18,... | collective-permute-start | bytes 147464 | tf_op jit(solution)/shard_map/ppermute | solution.py:500
  13.7 5.1 %collective-permute-start.2 = (f32[72,128]{1,0:T(8,128)S(1)}, f32[72,128]{1,0:T(8,128)S(1)}, u32[]{:S(2)}, u32[]{:S(2)}) collective-permute-start(f32[72,128]{1,0:T(8,128)S(1)} %get-tuple-element.44), channel_id=1, source_target_pairs={{0,4},{8,12},{4,0},{12,8},{1,5},{9,13},{5,1},{13,9},{2,6},{10,14},... | collective-permute-start | bytes 110600 | tf_op jit(solution)/shard_map/ppermute | solution.py:499
  15.6 3.1 %collective-permute-start.3 = (f32[72,128]{1,0:T(8,128)S(1)}, f32[72,128]{1,0:T(8,128)S(1)}, u32[]{:S(2)}, u32[]{:S(2)}) collective-permute-start(f32[72,128]{1,0:T(8,128)S(1)} %get-tuple-element.45), channel_id=1, source_target_pairs={{4,8},{8,4},{5,9},{9,5},{6,10},{10,6},{7,11},{11,7},{20,24},{24,20... | collective-permute-start | bytes 110600 | tf_op jit(solution)/shard_map/ppermute | solution.py:498
